TPU v7x, 32 devices: a whole 2x2x4 slice. The times are simulated.
32 devices in a mesh: blk: 4 (over y, core), order: 8 (over z, x).
Axes of the slice: x: 2, y: 2, z: 4, core: 2. Of those that a mesh axis runs over, the one named last changes fastest.
Arguments:
- sky_maps: float32 [16, 64, 8192], P(None, ('blk', 'order')), may hold values from -6 to 6
- wigner_d: bfloat16 [64, 1536, 2048], P(None, 'blk', 'order'), may hold values from -0.75 to 0.75
- order_of_slot: int32 [2048], replicated, may hold values from 0 to 2047, each once
- kernel: float32 [8, 2, 1536], P(None, None, 'blk'), may hold values from -6 to 6
Outputs:
- wavelet_coef: bfloat16 [8, 16, 2, 1536, 2048], P(None, None, None, 'blk', 'order')
Inputs may be any that keep to these rules, and one draw needn't show every extreme that they name: `order_of_slot`: every order appears in exactly one slot.
All inputs are finite; a program needn't handle non-finite values.
Results may differ from a plain program's by a relative error of at most 0.0049.
Values may be sent and summed in bfloat16 or wider, within the bound.
No kernel may reach another device: no remote copies, remote signals or barrier semaphores. Data moves between devices by JAX's collectives and lax.ppermute only.
A program may use at most 192 MiB of HBM per device.

v0:
```python
import math

import jax
import jax.numpy as jnp
from jax import lax
from jax.sharding import PartitionSpec as P

DEG_LO = 512


HIGHEST = lax.Precision.HIGHEST
RADIX = 128


def cycle_spectrum(sky_maps, orders):
    maps_count = sky_maps.shape[0]
    cycle_count = sky_maps.shape[1]
    samples = sky_maps.shape[2]
    outer_len = samples // RADIX
    order_blocks = orders // RADIX
    values = sky_maps.reshape(maps_count, cycle_count, RADIX, outer_len)
    inner_idx = jnp.arange(RADIX, dtype=jnp.int32)
    outer_idx = jnp.arange(outer_len, dtype=jnp.int32)
    block_idx = jnp.arange(order_blocks, dtype=jnp.int32)
    inner_angle = (
        2.0
        * math.pi
        / RADIX
        * (inner_idx[:, None] * inner_idx[None, :] % RADIX).astype(jnp.float32)
    )
    inner_re = jnp.einsum("abkj,km->abjm", values, jnp.cos(inner_angle), precision=HIGHEST)
    inner_im = -jnp.einsum("abkj,km->abjm", values, jnp.sin(inner_angle), precision=HIGHEST)
    twist_angle = (
        2.0 * math.pi / samples * (outer_idx[:, None] * inner_idx[None, :]).astype(jnp.float32)
    )
    twist_cos = jnp.cos(twist_angle)
    twist_sin = jnp.sin(twist_angle)
    turned_re = inner_re * twist_cos + inner_im * twist_sin
    turned_im = inner_im * twist_cos - inner_re * twist_sin
    outer_angle = (
        2.0
        * math.pi
        / outer_len
        * (block_idx[:, None] * outer_idx[None, :] % outer_len).astype(jnp.float32)
    )
    outer_cos = jnp.cos(outer_angle)
    outer_sin = jnp.sin(outer_angle)
    final_re = jnp.einsum("abjm,ij->abim", turned_re, outer_cos, precision=HIGHEST) + jnp.einsum(
        "abjm,ij->abim", turned_im, outer_sin, precision=HIGHEST
    )
    final_im = jnp.einsum("abjm,ij->abim", turned_im, outer_cos, precision=HIGHEST) - jnp.einsum(
        "abjm,ij->abim", turned_re, outer_sin, precision=HIGHEST
    )
    factor = 1.0 / math.sqrt(samples)
    stacked = jnp.stack(
        [
            final_re.reshape(maps_count, cycle_count, orders),
            final_im.reshape(maps_count, cycle_count, orders),
        ],
        axis=0,
    )
    return (stacked * factor).astype(jnp.bfloat16)


def add_cycles(piece, table):
    term = jnp.einsum("mrcs,rjs->mcjs", piece, table, preferred_element_type=jnp.float32)
    return term


def local(sky_maps, wigner_d, order_of_slot, kernel):
    orders = order_of_slot.shape[0]
    deg_count = wigner_d.shape[1]
    slot_count = wigner_d.shape[2]
    maps_count = sky_maps.shape[0]
    cycle_count = sky_maps.shape[1]
    groups = lax.axis_size("order")
    cycle_groups = lax.axis_size("blk")
    spectrum = cycle_spectrum(sky_maps, orders)
    slot_table = order_of_slot.reshape(groups, slot_count)
    order_ids = jnp.arange(orders, dtype=jnp.int32)
    one_hot = (order_ids[:, None, None] == slot_table[None, :, :]).astype(jnp.bfloat16)
    by_owner = jnp.einsum(
        "cmro,ogs->mgrcs", spectrum, one_hot, preferred_element_type=jnp.float32
    ).astype(jnp.bfloat16)
    copies = jnp.broadcast_to(
        by_owner[:, None], (maps_count, cycle_groups, groups, cycle_count, 2, slot_count)
    )
    copies = copies.reshape(maps_count, cycle_groups * groups * cycle_count, 2, slot_count)
    every_cycle = lax.all_to_all(copies, ("blk", "order"), split_axis=1, concat_axis=1, tiled=True)
    harmonic = add_cycles(every_cycle, wigner_d)
    my_orders = lax.dynamic_slice_in_dim(
        order_of_slot, lax.axis_index("order") * slot_count, slot_count, 0
    )
    degree = DEG_LO + lax.axis_index("blk") * deg_count + jnp.arange(deg_count, dtype=jnp.int32)
    live = degree[:, None] >= my_orders[None, :]
    real_part = jnp.where(live[None], harmonic[:, 0], 0.0)[None, :, None]
    imag_part = jnp.where(live[None], harmonic[:, 1], 0.0)[None, :, None]
    kern_re = kernel[:, 0, :]
    kern_im = kernel[:, 1, :]
    first = jnp.stack([kern_re, -kern_im], axis=1)[:, None, :, :, None]
    second = jnp.stack([kern_im, kern_re], axis=1)[:, None, :, :, None]
    return (real_part * first + imag_part * second).astype(jnp.bfloat16)


def solution(mesh):
    return jax.shard_map(
        local,
        mesh=mesh,
        in_specs=(
            P(None, ("blk", "order"), None),
            P(None, "blk", "order"),
            P(),
            P(None, None, "blk"),
        ),
        out_specs=P(None, None, None, "blk", "order"),
        check_vma=False,
    )
```

profile of v0, /device:TPU:0, one launch (start us, length us, event | category | flops | bytes accessed | tf_op | source)
XLA Modules:
  0.0 104.0 jit_solution(6579013343517247745)
XLA Ops:
  0.0 0.1 fusion.31
  0.1 2.3 %reshape.86 = f32[16,2,128,64]{3,2,1,0:T(8,128)S(1)} reshape(f32[16,2,8192]{2,1,0:T(2,128)} %param.4) | data formatting | bytes 2097152 | tf_op jit(solution)/shard_map/reshape | solution.py:21
  2.4 0.0 copy-start
  2.5 1.3 %copy-done = f32[16,2,128,64]{3,2,1,0:T(8,128)} copy-done((f32[16,2,128,64]{3,2,1,0:T(8,128)}, f32[16,2,128,64]{3,2,1,0:T(8,128)S(1)}, u32[]{:S(2)}) %copy-start) | copy-done | bytes 1048600
  3.8 0.0 copy-start.2
  3.8 3.5 %convolution_bitcast_fusion.1 = f32[16,2,64,128]{3,2,1,0:T(8,128)S(1)} fusion(f32[16,2,128,64]{3,2,1,0:T(8,128)S(1)} %reshape.86), kind=kOutput, calls=%fused_computation.12 | convolution fusion | flops 402882560 | bytes 2097152 | tf_op jit(solution)/shard_map/abkj,km->abjm/dot_general | solution.py:31
  7.3 5.1 %fusion.6 = f32[16,2,64,128]{3,2,1,0:T(8,128)S(1)} fusion(f32[16,2,128,64]{3,2,1,0:T(8,128)} %copy-done), kind=kOutput, calls=%fused_computation.11 | convolution fusion | flops 403144704 | bytes 2097152 | tf_op jit(solution)/shard_map/abkj,km->abjm/dot_general | solution.py:32
  12.3 0.7 fusion.17
  13.1 0.7 fusion.16
  13.9 0.0 copy-done.2
  13.9 0.8 fusion.10
  14.6 0.1 stack_reshape.7
  14.8 0.2 copy.29
  14.9 0.8 fusion.11
  15.7 0.1 stack_reshape.6
  15.9 0.2 copy.28
  16.0 3.2 %fusion.12 = bf16[16,8,2,2,256]{4,0,2,3,1:T(8,128)(2,1)S(1)} fusion(s32[8,256]{1,0:T(8,128)S(1)} %eq.20, f32[1,16,2,2048]{3,1,2,0:T(8,128)S(1)} %copy.29, f32[1,16,2,2048]{3,1,2,0:T(8,128)S(1)} %copy.28), kind=kOutput, calls=%fused_computation.18 | convolution fusion | flops 541589504 | bytes 794624 | tf_op jit(solution)/shard_map/cmro,ogs->mgrcs/dot_general | solution.py:82
  19.3 1.1 %broadcast_in_dim.15 = bf16[16,4,8,2,2,256]{5,0,4,3,2,1:T(8,128)(2,1)} broadcast(bf16[16,8,2,2,256]{4,0,3,2,1:T(8,128)(2,1)S(1)} %copy.30), dimensions={0,2,3,4,5} | broadcast | bytes 1310720 | tf_op jit(solution)/shard_map/broadcast_in_dim | solution.py:85
  20.4 7.3 %all-to-all-start = ((bf16[16,64,2,256]{3,0,2,1:T(8,128)(2,1)}), bf16[16,64,2,256]{3,0,2,1:T(8,128)(2,1)S(1)}, u32[]{:S(2)}, u32[]{:S(2)}) async-start(bf16[16,64,2,256]{3,0,2,1:T(8,128)(2,1)} %bitcast.18), calls=%async_computation | async-start | bytes 2097152 | tf_op jit(solution)/shard_map/all_to_all | solution.py:89
  27.7 0.1 dynamic_slice.3
  27.8 0.0 copy-start.1
  27.8 16.5 %copy.43 = bf16[64,384,256,1]{1,0,3,2:T(8,128)(2,1)} copy(bf16[64,384,256,1]{2,1,0,3:T(8,128)(2,1)} %bitcast.68) | data formatting | bytes 25165824 | tf_op args[1]
  44.3 0.0 copy-done.1
  44.4 0.1 broadcast_compare_fusion
  44.5 10.8 %all-to-all-done = bf16[16,64,2,256]{3,0,2,1:T(8,128)(2,1)S(1)} async-done(((bf16[16,64,2,256]{3,0,2,1:T(8,128)(2,1)}), bf16[16,64,2,256]{3,0,2,1:T(8,128)(2,1)S(1)}, u32[]{:S(2)}, u32[]{:S(2)}) %all-to-all-start) | async-done | bytes 1048608 | tf_op jit(solution)/shard_map/all_to_all | solution.py:89
  55.3 3.5 %copy.31 = bf16[16,64,2,256]{1,0,2,3:T(8,128)(2,1)S(1)} copy(bf16[16,64,2,256]{3,0,2,1:T(8,128)(2,1)S(1)} %all-to-all-done) | data formatting | bytes 2097152 | tf_op jit(solution)/shard_map/all_to_all | solution.py:89
  58.8 5.9 %convolution_bitcast_fusion = f32[16,2,384,256]{2,0,1,3:T(8,128)S(1)} fusion(bf16[16,64,2,256]{1,0,2,3:T(8,128)(2,1)S(1)} %copy.31, bf16[64,384,256,1]{1,0,3,2:T(8,128)(2,1)} %copy.43), kind=kOutput, calls=%fused_computation.9 | convolution fusion | flops 402653184 | bytes 26214400 | tf_op jit(solution)/shard_map/mrcs,rjs->mcjs/dot_general | solution.py:66
  64.7 5.4 %fusion.5 = (f32[16,384,256]{1,0,2:T(8,128)}, f32[16,384,256]{1,0,2:T(8,128)}) fusion(f32[16,2,384,256]{2,0,1,3:T(8,128)S(1)} %convolution_bitcast_fusion, pred[384,256]{0,1:T(8,128)(4,1)S(1)} %broadcast_compare_fusion), kind=kLoop, calls=%fused_computation.8 | loop fusion | flops 3145728 | bytes 25264128 | tf_op jit(solution)/shard_map/jit(_where)/select_n | solution.py:96
  70.1 6.6 %copy.34 = f32[16,384,256]{2,1,0:T(8,128)} copy(f32[16,384,256]{1,0,2:T(8,128)} %get-tuple-element.5) | data formatting | bytes 12582912 | tf_op jit(solution)/shard_map/jit(_where)/select_n | solution.py:96
  76.7 6.6 %copy.35 = f32[16,384,256]{2,1,0:T(8,128)} copy(f32[16,384,256]{1,0,2:T(8,128)} %get-tuple-element.6) | data formatting | bytes 12582912 | tf_op jit(solution)/shard_map/jit(_where)/select_n | solution.py:97
  83.3 20.6 %add_convert_fusion = bf16[8,16,2,384,256]{4,3,2,1,0:T(8,128)(2,1)} fusion(f32[8,2,384]{2,1,0:T(2,128)S(1)} %get-tuple-element.11, f32[16,384,256]{2,1,0:T(8,128)} %copy.35, f32[8,2,384]{2,1,0:T(2,128)S(1)} %get-tuple-element.10, f32[16,384,256]{2,1,0:T(8,128)} %copy.34), kind=kLoop, calls=%fused_computation | loop fusion | flops 100663296 | bytes 62963712 | tf_op jit(solution)/shard_map/convert_element_type | solution.py:102
  (5 shorter events, 0.1 us)
Async XLA Ops:
  2.4 1.3 %copy-start = (f32[16,2,128,64]{3,2,1,0:T(8,128)}, f32[16,2,128,64]{3,2,1,0:T(8,128)S(1)}, u32[]{:S(2)}) copy-start(f32[16,2,128,64]{3,2,1,0:T(8,128)S(1)} %reshape.86) | copy-start | bytes 3145732
  3.8 10.1 %copy-start.2 = (s32[2048]{0:T(1024)S(1)}, s32[2048]{0:T(1024)}, u32[]{:S(2)}) copy-start(s32[2048]{0:T(1024)} %param.6) | copy-start | bytes 24580
  20.4 34.9 %all-to-all-start = ((bf16[16,64,2,256]{3,0,2,1:T(8,128)(2,1)}), bf16[16,64,2,256]{3,0,2,1:T(8,128)(2,1)S(1)}, u32[]{:S(2)}, u32[]{:S(2)}) async-start(bf16[16,64,2,256]{3,0,2,1:T(8,128)(2,1)} %bitcast.18), calls=%async_computation | async-start | bytes 2097152 | tf_op jit(solution)/shard_map/all_to_all | solution.py:89
  27.8 16.5 %copy-start.1 = (f32[8,2,384]{2,1,0:T(2,128)S(1)}, f32[8,2,384]{2,1,0:T(2,128)}, u32[]{:S(2)}) copy-start(f32[8,2,384]{2,1,0:T(2,128)} %param.7) | copy-start | bytes 73732
where the time goes:
time: 105 us; the launch traced here: 104 us
  local copies, waits for them, and re-layouts  38.7 us (37%)
  other arithmetic  26.3 us (25%)
  matrix products  20.6 us (20%)
  waiting for transfers between devices  10.8 us (10%)
  starting transfers between devices  7.3 us (7%)
    convert_element_type x1, other arithmetic, local(): return (real_part * first + imag_part * second).astype(jnp.bfloat16)  20.6 us
    unnamed x7, local copies, waits for them, and re-layouts  17.8 us
    all_to_all x1, waiting for transfers between devices, local(): lax.all_to_all(copies, ('blk', 'order'), split_axis=1, concat_axis=1, til...  10.8 us
    all_to_all x1, starting transfers between devices, local(): lax.all_to_all(copies, ('blk', 'order'), split_axis=1, concat_axis=1, til...  7.3 us
    select_n x1, local copies, waits for them, and re-layouts, local(): real_part = jnp.where(live[None], harmonic[:, 0], 0.0)[None, :, None]  6.61 us
    select_n x1, local copies, waits for them, and re-layouts, local(): imag_part = jnp.where(live[None], harmonic[:, 1], 0.0)[None, :, None]  6.6 us
    dot_general x1, matrix products, add_cycles(): jnp.einsum('mrcs,rjs->mcjs', piece, table, preferred_element_type=jnp.flo...  5.86 us
    select_n x1, other arithmetic, local(): real_part = jnp.where(live[None], harmonic[:, 0], 0.0)[None, :, None]  5.4 us
  transfers between devices with their start and end apart: 1, of which 1 were waited for; matrix products, arithmetic and copies ran while one was open for 16% of the time, Pallas kernels for 0%

commit v1 on v0

--- a/solution.py
+++ b/solution.py
@@ -3,13 +3,19 @@
 import jax
 import jax.numpy as jnp
 from jax import lax
+from jax.experimental import pallas as pl
+from jax.experimental.pallas import tpu as pltpu
 from jax.sharding import PartitionSpec as P
 
 DEG_LO = 512
 
 
+F32 = jnp.float32
+BF16 = jnp.bfloat16
 HIGHEST = lax.Precision.HIGHEST
 RADIX = 128
+PLACE_UNROLL = 8
+MULT_UNROLL = 4
 
 
 def cycle_spectrum(sky_maps, orders):
@@ -62,44 +68,204 @@
     return (stacked * factor).astype(jnp.bfloat16)
 
 
-def add_cycles(piece, table):
-    term = jnp.einsum("mrcs,rjs->mcjs", piece, table, preferred_element_type=jnp.float32)
-    return term
+def table_body(src_ref, base_ref, ids_ref, kern_ref, wig_ref, out_ref, wide_ref):
+    rows, degs, slots = wig_ref.shape
+
+    @pl.when(pl.program_id(0) == 0)
+    def _():
+        columns = kern_ref[...].T
+        for i in range(wide_ref.shape[0]):
+            wide_ref[i] = jnp.broadcast_to(columns[:, i : i + 1], (degs, slots)).astype(BF16)
+
+    degree = base_ref[0] + lax.broadcasted_iota(jnp.int32, (slots, degs), 1)
+    live = degree >= ids_ref[...]
+
+    def turned(row):
+        flat = wig_ref[row].astype(F32).T
+        return jnp.where(live, flat, 0.0).reshape(slots // 8, 8, degs)
+
+    for row in range(0, rows, 2):
+        pair = jnp.concatenate([turned(row), turned(row + 1)], axis=1)
+        out_ref[:, row // 2] = pair.astype(BF16)
+
+
+def make_table(wigner_d, my_orders, base, source, kern, step):
+    cycles, degs, slots = wigner_d.shape
+    count = kern.shape[0]
+    return pl.pallas_call(
+        table_body,
+        grid_spec=pltpu.PrefetchScalarGridSpec(
+            num_scalar_prefetch=2,
+            grid=(cycles // step,),
+            in_specs=[
+                pl.BlockSpec((slots, 1), lambda i, src, base: (0, 0)),
+                pl.BlockSpec((count, degs), lambda i, src, base: (0, 0)),
+                pl.BlockSpec((step, degs, slots), lambda i, src, base: (src[i], 0, 0)),
+            ],
+            out_specs=[
+                pl.BlockSpec((slots // 8, step // 2, 16, degs), lambda i, src, base: (0, i, 0, 0)),
+                pl.BlockSpec((count, degs, slots), lambda i, src, base: (0, 0, 0)),
+            ],
+        ),
+        out_shape=[
+            jax.ShapeDtypeStruct((slots // 8, cycles // 2, 16, degs), BF16),
+            jax.ShapeDtypeStruct((count, degs, slots), BF16),
+        ],
+        compiler_params=pltpu.CompilerParams(vmem_limit_bytes=40 << 20),
+        cost_estimate=pl.CostEstimate(
+            flops=cycles * degs * slots * 16, bytes_accessed=cycles * degs * slots * 4, transcendentals=0
+        ),
+        name="table",
+    )(source, base, my_orders.reshape(slots, 1), kern, wigner_d)
+
+
+def final_body(*refs):
+    pieces = len(refs) - 10
+    parts = refs[:pieces]
+    tab_hbm, wide_hbm, out_ref, xs, dp, ht, ab, wide_ref, tab_ref, sem = refs[pieces:]
+    rows, lines, slots = parts[0].shape
+    cycles = rows * pieces
+    groups = slots // 8
+    degs = tab_ref.shape[3]
+    depth = cycles * 8
+    count = out_ref.shape[0]
+    halves = slots // 128
+    m = pl.program_id(0)
+    chunks = sem.shape[0] - 1
+    span = groups // chunks
+
+    def fetch(i):
+        part = pl.ds(i * span, span)
+        return pltpu.make_async_copy(tab_hbm.at[part], tab_ref.at[part], sem.at[i])
+
+    fetch_wide = pltpu.make_async_copy(wide_hbm, wide_ref, sem.at[chunks])
+
+    @pl.when(m == 0)
+    def _():
+        for i in range(chunks):
+            fetch(i).start()
+        fetch_wide.start()
+        for d in range(pieces):
+            for h in range(halves):
+                block = parts[d][:, :, h * 128 : (h + 1) * 128].astype(F32)
+                xs[h, pl.ds(d * rows * lines, rows * lines), :] = block.reshape(rows * lines, 128)
+        spread = (
+            lax.broadcasted_iota(jnp.int32, (cycles, depth), 0)
+            == lax.broadcasted_iota(jnp.int32, (cycles, depth), 1) // 8
+        ).astype(BF16)
+        keep = (lax.broadcasted_iota(jnp.int32, (128, depth), 0) % 8) == (
+            lax.broadcasted_iota(jnp.int32, (128, depth), 1) % 8
+        )
+
+        def place(i, carry):
+            for h in range(halves):
+                pair = []
+                for t in range(2):
+                    x = xs[h, pl.ds(2 * i + t, cycles, stride=lines), :].astype(BF16)
+                    f = lax.dot_general(
+                        x, spread, (((0,), (0,)), ((), ())), preferred_element_type=F32
+                    )
+                    pair.append(jnp.where(keep, f, 0.0).reshape(16, 8, depth))
+                dp[h * 16 : (h + 1) * 16, i] = jnp.concatenate(pair, axis=1).astype(BF16)
+            return carry
+
+        lax.fori_loop(0, lines // 2, place, 0, unroll=PLACE_UNROLL)
+
+        def multiply(g, carry):
+            product = jnp.dot(
+                dp[g].reshape(lines * 8, depth),
+                tab_ref[g].reshape(depth, degs),
+                preferred_element_type=F32,
+            )
+            ht[:, pl.ds(pl.multiple_of(g * 8, 8), 8), :] = product.reshape(lines, 8, degs)
+            return carry
+
+        for i in range(chunks):
+            fetch(i).wait()
+            lax.fori_loop(i * span, (i + 1) * span, multiply, 0, unroll=MULT_UNROLL)
+        fetch_wide.wait()
+
+    for c in range(2):
+        turned = [ht[2 * m + c, h * 128 : (h + 1) * 128, :].T for h in range(halves)]
+        ab[c] = jnp.concatenate(turned, axis=1).astype(BF16)
+    for top in range(0, degs, 16):
+        js = slice(top, top + 16)
+        a = ab[0, js, :]
+        b = ab[1, js, :]
+        for n in range(count):
+            p = wide_ref[2 * n, js, :]
+            q = wide_ref[2 * n + 1, js, :]
+            out_ref[n, 0, 0, js, :] = (a * p + b * q).astype(BF16)
+            out_ref[n, 0, 1, js, :] = (b * p - a * q).astype(BF16)
+
+
+def combine(parts, table, wide):
+    rows, lines, slots = parts[0].shape
+    cycles = rows * len(parts)
+    degs = table.shape[3]
+    count = wide.shape[0] // 2
+    maps_count = lines // 2
+    once = pl.BlockSpec(parts[0].shape, lambda m: (0, 0, 0), pipeline_mode=pl.Buffered(1))
+    return pl.pallas_call(
+        final_body,
+        grid=(maps_count,),
+        in_specs=[once] * len(parts) + [pl.BlockSpec(memory_space=pl.ANY)] * 2,
+        out_specs=pl.BlockSpec((count, 1, 2, degs, slots), lambda m: (0, m, 0, 0, 0)),
+        out_shape=jax.ShapeDtypeStruct((count, maps_count, 2, degs, slots), BF16),
+        scratch_shapes=[
+            pltpu.VMEM((slots // 128, cycles * lines, 128), F32),
+            pltpu.VMEM((slots // 8, maps_count, 16, cycles * 8), BF16),
+            pltpu.VMEM((lines, slots, degs), F32),
+            pltpu.VMEM((2, degs, slots), BF16),
+            pltpu.VMEM(wide.shape, BF16),
+            pltpu.VMEM(table.shape, BF16),
+            pltpu.SemaphoreType.DMA((5,)),
+        ],
+        compiler_params=pltpu.CompilerParams(vmem_limit_bytes=60 << 20),
+        name="combine",
+    )(*parts, table, wide)
 
 
 def local(sky_maps, wigner_d, order_of_slot, kernel):
     orders = order_of_slot.shape[0]
-    deg_count = wigner_d.shape[1]
-    slot_count = wigner_d.shape[2]
-    maps_count = sky_maps.shape[0]
-    cycle_count = sky_maps.shape[1]
+    cycles, deg_count, slot_count = wigner_d.shape
+    maps_count, cycle_count, _ = sky_maps.shape
     groups = lax.axis_size("order")
     cycle_groups = lax.axis_size("blk")
+    me = lax.axis_index("blk")
+    my_orders = lax.dynamic_slice_in_dim(
+        order_of_slot, lax.axis_index("order") * slot_count, slot_count, 0
+    )
+
+    bits = []
+    bit = cycle_groups // 2
+    while bit:
+        bits.append(bit)
+        bit //= 2
+    masks = [0]
+    for bit in bits:
+        masks = masks + [mask ^ bit for mask in masks]
+    step = 8
+    per = groups * cycle_count // step
+    piece = jnp.asarray(masks, dtype=jnp.int32) ^ me
+    source = (piece[:, None] * per + jnp.arange(per, dtype=jnp.int32)[None, :]).reshape(-1)
+    base = (DEG_LO + me * deg_count).astype(jnp.int32).reshape(1)
+    flat_kernel = kernel.reshape(-1, deg_count)
+    table, wide = make_table(wigner_d, my_orders, base, source, flat_kernel, step)
+
     spectrum = cycle_spectrum(sky_maps, orders)
     slot_table = order_of_slot.reshape(groups, slot_count)
     order_ids = jnp.arange(orders, dtype=jnp.int32)
-    one_hot = (order_ids[:, None, None] == slot_table[None, :, :]).astype(jnp.bfloat16)
+    one_hot = (order_ids[:, None, None] == slot_table[None, :, :]).astype(BF16)
     by_owner = jnp.einsum(
-        "cmro,ogs->mgrcs", spectrum, one_hot, preferred_element_type=jnp.float32
-    ).astype(jnp.bfloat16)
-    copies = jnp.broadcast_to(
-        by_owner[:, None], (maps_count, cycle_groups, groups, cycle_count, 2, slot_count)
-    )
-    copies = copies.reshape(maps_count, cycle_groups * groups * cycle_count, 2, slot_count)
-    every_cycle = lax.all_to_all(copies, ("blk", "order"), split_axis=1, concat_axis=1, tiled=True)
-    harmonic = add_cycles(every_cycle, wigner_d)
-    my_orders = lax.dynamic_slice_in_dim(
-        order_of_slot, lax.axis_index("order") * slot_count, slot_count, 0
-    )
-    degree = DEG_LO + lax.axis_index("blk") * deg_count + jnp.arange(deg_count, dtype=jnp.int32)
-    live = degree[:, None] >= my_orders[None, :]
-    real_part = jnp.where(live[None], harmonic[:, 0], 0.0)[None, :, None]
-    imag_part = jnp.where(live[None], harmonic[:, 1], 0.0)[None, :, None]
-    kern_re = kernel[:, 0, :]
-    kern_im = kernel[:, 1, :]
-    first = jnp.stack([kern_re, -kern_im], axis=1)[:, None, :, :, None]
-    second = jnp.stack([kern_im, kern_re], axis=1)[:, None, :, :, None]
-    return (real_part * first + imag_part * second).astype(jnp.bfloat16)
+        "cmro,ogs->grmcs", spectrum, one_hot, preferred_element_type=F32
+    ).astype(BF16)
+    by_owner = by_owner.reshape(groups * cycle_count, maps_count * 2, slot_count)
+    parts = [lax.all_to_all(by_owner, "order", split_axis=0, concat_axis=0, tiled=True)]
+    for bit in bits:
+        pairs = [(i, i ^ bit) for i in range(cycle_groups)]
+        parts = parts + [lax.ppermute(part, "blk", pairs) for part in parts]
+    return combine(parts, table, wide)
 
 
 def solution(mesh):

time: 105 us -> 92.5 us (0.88)
  Pallas kernels: 0 us -> 47.1 us
  local copies, waits for them, and re-layouts: 38.7 us -> 7.35 us
  other arithmetic: 26.3 us -> 0.21 us
  blocking collectives: 0 us -> 16 us
  waiting for transfers between devices: 10.8 us -> 4.86 us
  matrix products: 20.6 us -> 14.8 us
  starting transfers between devices: 7.3 us -> 1.52 us
    pallas_call x0 -> x2, Pallas kernels: none -> 47.1 us  [the longest x1 32.6 us: combine(): pl.pallas_call(final_body, grid=(maps_count,), in_specs=[once] * len(part...]
    convert_element_type x1 -> x0, other arithmetic: 20.6 us -> none  [local(): return (real_part * first + imag_part * second).astype(jnp.bfloat16)]
    all_to_all x0 -> x1, blocking collectives: none -> 16 us  [local(): lax.all_to_all(by_owner, 'order', split_axis=0, concat_axis=0, tiled=True)]
    unnamed x7 -> x18, local copies, waits for them, and re-layouts: 17.8 us -> 3.77 us
    select_n x2 -> x0, local copies, waits for them, and re-layouts: 13.2 us -> none  [the longest x1 6.61 us: local(): real_part = jnp.where(live[None], harmonic[:, 0], 0.0)[None, :, None]]
    all_to_all x1 -> x0, waiting for transfers between devices: 10.8 us -> none  [local(): lax.all_to_all(copies, ('blk', 'order'), split_axis=1, concat_axis=1, til...]
    all_to_all x1 -> x0, starting transfers between devices: 7.3 us -> none  [local(): lax.all_to_all(copies, ('blk', 'order'), split_axis=1, concat_axis=1, til...]
    dot_general x2 -> x1, matrix products: 9.07 us -> 3.22 us  [local(): jnp.einsum('cmro,ogs->grmcs', spectrum, one_hot, preferred_element_type=F32)]
  transfers between devices with their start and end apart: 1 -> 3, of which waited for: 1 -> 1; matrix products, arithmetic and copies ran while one was open for 16% -> 0% of each run, Pallas kernels for 0% -> 16%
where the time goes in v1:
time: 92.5 us; the launch traced here: 92.2 us
  Pallas kernels  47.1 us (51%)
  blocking collectives  16 us (17%)
  matrix products  14.8 us (16%)
  local copies, waits for them, and re-layouts  7.35 us (8%)
  waiting for transfers between devices  4.86 us (5%)
  starting transfers between devices  1.52 us (2%)
    pallas_call x1, Pallas kernels, combine(): pl.pallas_call(final_body, grid=(maps_count,), in_specs=[once] * len(part...  32.6 us
    all_to_all x1, blocking collectives, local(): lax.all_to_all(by_owner, 'order', split_axis=0, concat_axis=0, tiled=True)  16 us
    pallas_call x1, Pallas kernels, make_table(): pl.pallas_call(table_body, grid_spec=pltpu.PrefetchScalarGridSpec(num_sca...  14.5 us
    dot_general x1, matrix products, cycle_spectrum(): jnp.einsum('abkj,km->abjm', values, jnp.sin(inner_angle), precision=HIGHEST)  5.08 us
    ppermute x3, waiting for transfers between devices, local(): parts = parts + [lax.ppermute(part, 'blk', pairs) for part in parts]  4.86 us
    unnamed x18, local copies, waits for them, and re-layouts  3.77 us
    dot_general x1, matrix products, cycle_spectrum(): jnp.einsum('abkj,km->abjm', values, jnp.cos(inner_angle), precision=HIGHEST)  3.49 us
    dot_general x1, matrix products, local(): jnp.einsum('cmro,ogs->grmcs', spectrum, one_hot, preferred_element_type=F32)  3.22 us
  transfers between devices with their start and end apart: 3, of which 1 were waited for; matrix products, arithmetic and copies ran while one was open for 0% of the time, Pallas kernels for 16%

profile of v1, /device:TPU:0, one launch (start us, length us, event | category | flops | bytes accessed | tf_op | source)
XLA Modules:
  0.0 92.2 jit_solution(5739761352542793997)
XLA Ops:
  0.0 0.1 fusion.29
  0.1 2.3 %reshape.58 = f32[16,2,128,64]{3,2,1,0:T(8,128)S(1)} reshape(f32[16,2,8192]{2,1,0:T(2,128)} %param.5) | data formatting | bytes 2097152 | tf_op jit(solution)/shard_map/reshape | solution.py:27
  2.4 0.0 copy-start.1
  2.5 1.3 %copy-done.1 = f32[16,2,128,64]{3,2,1,0:T(8,128)} copy-done((f32[16,2,128,64]{3,2,1,0:T(8,128)}, f32[16,2,128,64]{3,2,1,0:T(8,128)S(1)}, u32[]{:S(2)}) %copy-start.1) | copy-done | bytes 1048600
  3.8 3.5 %convolution_bitcast_fusion = f32[16,2,64,128]{3,2,1,0:T(8,128)S(1)} fusion(f32[16,2,128,64]{3,2,1,0:T(8,128)S(1)} %reshape.58), kind=kOutput, calls=%fused_computation.6 | convolution fusion | flops 402882560 | bytes 2097152 | tf_op jit(solution)/shard_map/abkj,km->abjm/dot_general | solution.py:37
  7.3 5.1 %fusion.4 = f32[16,2,64,128]{3,2,1,0:T(8,128)S(1)} fusion(f32[16,2,128,64]{3,2,1,0:T(8,128)} %copy-done.1), kind=kOutput, calls=%fused_computation.5 | convolution fusion | flops 403144704 | bytes 2097152 | tf_op jit(solution)/shard_map/abkj,km->abjm/dot_general | solution.py:38
  12.3 0.0 copy-start.7
  12.4 0.7 fusion.15
  13.1 0.7 fusion.14
  13.9 0.0 copy-done.7
  13.9 0.8 fusion.8
  14.7 0.1 stack_reshape.7
  14.8 0.2 copy.15
  15.0 0.8 fusion.9
  15.7 0.1 stack_reshape.6
  15.9 0.2 copy.14
  16.0 0.0 copy-start.8
  16.0 0.0 copy-start.6
  16.1 3.2 %fusion.10 = bf16[8,2,16,2,256]{4,2,1,3,0:T(8,128)(2,1)S(1)} fusion(s32[8,256]{1,0:T(8,128)S(1)} %eq.20, f32[1,16,2,2048]{3,1,2,0:T(8,128)S(1)} %copy.15, f32[1,16,2,2048]{3,1,2,0:T(8,128)S(1)} %copy.14), kind=kOutput, calls=%fused_computation.12 | convolution fusion | flops 541589504 | bytes 794624 | tf_op jit(solution)/shard_map/cmro,ogs->grmcs/dot_general | solution.py:260
  19.3 0.3 copy.16
  19.6 0.1 reshape.48
  19.7 16.0 %all_to_all.5.refs_0_ = bf16[16,32,256]{2,1,0:T(8,128)(2,1)S(1)} all-to-all(bf16[16,32,256]{2,1,0:T(8,128)(2,1)S(1)} %reshape.48), channel_id=1, replica_groups=mesh['blk'=4,'order'=8] {'order'}, dimensions={0} | all-to-all | bytes 524288 | tf_op jit(solution)/shard_map/all_to_all | solution.py:264
  35.6 0.0 copy-start.2
  35.6 1.5 %collective-permute-start = (bf16[16,32,256]{2,1,0:T(8,128)(2,1)S(1)}, bf16[16,32,256]{2,1,0:T(8,128)(2,1)S(1)}, u32[]{:S(2)}, u32[]{:S(2)}) collective-permute-start(bf16[16,32,256]{2,1,0:T(8,128)(2,1)S(1)} %all_to_all.5.refs_0_), channel_id=1, source_target_pairs={{0,16},{8,24},{16,0},{24,8},{1,17},{9,25},{17,1},{25,9},{2,18},{10... | collective-permute-start | bytes 786440 | tf_op jit(solution)/shard_map/ppermute | solution.py:267
  37.1 0.0 collective-permute-start.1
  37.2 4.8 %collective-permute-done.refs_1_ = bf16[16,32,256]{2,1,0:T(8,128)(2,1)S(1)} collective-permute-done((bf16[16,32,256]{2,1,0:T(8,128)(2,1)S(1)}, bf16[16,32,256]{2,1,0:T(8,128)(2,1)S(1)}, u32[]{:S(2)}, u32[]{:S(2)}) %collective-permute-start) | collective-permute-done | bytes 262176 | tf_op jit(solution)/shard_map/ppermute | solution.py:267
  42.0 0.0 copy-start.3
  42.0 0.0 collective-permute-start.2
  42.0 0.0 copy-done.8
  42.0 0.1 dynamic_slice.3
  42.1 0.1 iota_add_fusion
  42.2 0.1 add.57.src_ref
  42.3 0.0 copy-done.6
  42.3 0.1 copy.17.ids_ref
  42.4 14.5 %table.1 = (bf16[32,32,16,384]{3,2,1,0:T(8,128)(2,1)}, bf16[16,384,256]{2,1,0:T(8,128)(2,1)S(1)}) custom-call(s32[8]{0:T(128)S(1)} %add.57.src_ref, s32[1]{0:T(128)} %bitcast.18.base_ref, s32[256,1]{1,0:T(8,128)S(1)} %copy.17.ids_ref, f32[16,384]{1,0:T(8,128)S(1)} %reshape.51.kern_ref, bf16[64,384,256]{2,1,0:T(8,128)(2,1)} %wig_ref.1), custom_call_target="tpu_custom_call" | custom-call | flops 100663296 | bytes 25165824 | tf_op jit(solution)/shard_map/table/pallas_call | solution.py:95
  57.0 0.0 copy-done.2
  57.0 0.0 copy-done.3
  57.0 0.0 copy-start
  57.0 1.6 %copy-done = bf16[16,384,256]{2,1,0:T(8,128)(2,1)} copy-done((bf16[16,384,256]{2,1,0:T(8,128)(2,1)}, bf16[16,384,256]{2,1,0:T(8,128)(2,1)S(1)}, u32[]{:S(2)}) %copy-start) | copy-done | bytes 3145752
  58.6 0.0 collective-permute-done.1.refs_2_
  58.6 0.0 copy-start.4
  58.6 0.0 collective-permute-done.2.refs_3_
  58.6 0.0 copy-start.5
  58.6 0.7 copy-done.4
  59.3 0.1 copy-done.5
  59.4 32.6 %combine.1 = bf16[8,16,2,384,256]{4,3,2,1,0:T(8,128)(2,1)} custom-call(bf16[16,32,256]{2,1,0:T(8,128)(2,1)} %copy-done.2, bf16[16,32,256]{2,1,0:T(8,128)(2,1)} %copy-done.3, bf16[16,32,256]{2,1,0:T(8,128)(2,1)} %copy-done.4, bf16[16,32,256]{2,1,0:T(8,128)(2,1)} %copy-done.5, bf16[32,32,16,384]{3,2,1,0:T(8,128)(2,1)} %get-tuple-element.7.refs_4_, ...), custom_call_target="tpu_custom_call" | custom-call | tf_op jit(solution)/shard_map/combine/pallas_call | solution.py:209
  (3 shorter events, 0.0 us)
Async XLA Ops:
  2.4 1.3 %copy-start.1 = (f32[16,2,128,64]{3,2,1,0:T(8,128)}, f32[16,2,128,64]{3,2,1,0:T(8,128)S(1)}, u32[]{:S(2)}) copy-start(f32[16,2,128,64]{3,2,1,0:T(8,128)S(1)} %reshape.58) | copy-start | bytes 3145732
  12.3 1.5 %copy-start.7 = (s32[2048]{0:T(1024)S(1)}, s32[2048]{0:T(1024)}, u32[]{:S(2)}) copy-start(s32[2048]{0:T(1024)} %param.7) | copy-start | bytes 24580
  16.0 26.0 %copy-start.8 = (s32[4]{0:T(128)S(1)}, s32[4]{0:T(128)}, u32[]{:S(2)}) copy-start(s32[4]{0:T(128)} %constant.58.clone) | copy-start | bytes 52
  16.0 26.2 %copy-start.6 = (f32[8,2,384]{2,1,0:T(2,128)S(1)}, f32[8,2,384]{2,1,0:T(2,128)}, u32[]{:S(2)}) copy-start(f32[8,2,384]{2,1,0:T(2,128)} %param.8) | copy-start | bytes 73732
  35.6 21.3 %copy-start.2 = (bf16[16,32,256]{2,1,0:T(8,128)(2,1)}, bf16[16,32,256]{2,1,0:T(8,128)(2,1)S(1)}, u32[]{:S(2)}) copy-start(bf16[16,32,256]{2,1,0:T(8,128)(2,1)S(1)} %all_to_all.5.refs_0_) | copy-start | bytes 786436
  35.6 6.4 %collective-permute-start = (bf16[16,32,256]{2,1,0:T(8,128)(2,1)S(1)}, bf16[16,32,256]{2,1,0:T(8,128)(2,1)S(1)}, u32[]{:S(2)}, u32[]{:S(2)}) collective-permute-start(bf16[16,32,256]{2,1,0:T(8,128)(2,1)S(1)} %all_to_all.5.refs_0_), channel_id=1, source_target_pairs={{0,16},{8,24},{16,0},{24,8},{1,17},{9,25},{17,1},{25,9},{2,18},{10... | collective-permute-start | bytes 786440 | tf_op jit(solution)/shard_map/ppermute | solution.py:267
  37.1 21.5 %collective-permute-start.1 = (bf16[16,32,256]{2,1,0:T(8,128)(2,1)S(1)}, bf16[16,32,256]{2,1,0:T(8,128)(2,1)S(1)}, u32[]{:S(2)}, u32[]{:S(2)}) collective-permute-start(bf16[16,32,256]{2,1,0:T(8,128)(2,1)S(1)} %all_to_all.5.refs_0_), channel_id=1, source_target_pairs={{0,8},{8,0},{16,24},{24,16},{1,9},{9,1},{17,25},{25,17},{2,10},{10... | collective-permute-start | bytes 786440 | tf_op jit(solution)/shard_map/ppermute | solution.py:267
  42.0 15.0 %copy-start.3 = (bf16[16,32,256]{2,1,0:T(8,128)(2,1)}, bf16[16,32,256]{2,1,0:T(8,128)(2,1)S(1)}, u32[]{:S(2)}) copy-start(bf16[16,32,256]{2,1,0:T(8,128)(2,1)S(1)} %collective-permute-done.refs_1_) | copy-start | bytes 786436
  42.0 16.6 %collective-permute-start.2 = (bf16[16,32,256]{2,1,0:T(8,128)(2,1)S(1)}, bf16[16,32,256]{2,1,0:T(8,128)(2,1)S(1)}, u32[]{:S(2)}, u32[]{:S(2)}) collective-permute-start(bf16[16,32,256]{2,1,0:T(8,128)(2,1)S(1)} %collective-permute-done.refs_1_), channel_id=1, source_target_pairs={{0,8},{8,0},{16,24},{24,16},{1,9},{9,1},{17,25},{25,17},{2,10},{10... | collective-permute-start | bytes 786440 | tf_op jit(solution)/shard_map/ppermute | solution.py:267
  57.0 1.6 %copy-start = (bf16[16,384,256]{2,1,0:T(8,128)(2,1)}, bf16[16,384,256]{2,1,0:T(8,128)(2,1)S(1)}, u32[]{:S(2)}) copy-start(bf16[16,384,256]{2,1,0:T(8,128)(2,1)S(1)} %get-tuple-element.8.refs_5_) | copy-start | bytes 9437188
  58.6 0.7 copy-start.4
  58.6 0.8 copy-start.5

commit v2 on v1

v2 whole, which is shorter than its diff:
```python
import functools
import math

import jax
import jax.numpy as jnp
import numpy as np
from jax import lax
from jax.experimental import pallas as pl
from jax.experimental.pallas import tpu as pltpu
from jax.sharding import PartitionSpec as P

DEG_LO = 512
LANES = 128
F32 = jnp.float32
BF16 = jnp.bfloat16
PLACE_UNROLL = 8
MULT_UNROLL = 4


def split(value):
    high = value.astype(BF16)
    return high, (value - high.astype(F32)).astype(BF16)


def three_pass(left, right):
    out = jnp.dot(left[0], right[0], preferred_element_type=F32)
    out += jnp.dot(left[0], right[1], preferred_element_type=F32)
    return out + jnp.dot(left[1], right[0], preferred_element_type=F32)


def fourier_tables(samples, orders, cycle_count):
    outer = samples // LANES
    high = orders // outer
    a = np.arange(outer)
    b = np.arange(LANES)
    q = np.arange(high)
    first = 2.0 * np.pi * (np.outer(a, a) % outer) / outer
    eye = np.eye(cycle_count)
    cos_first = np.einsum("rs,pa->rpas", eye, np.cos(first))
    sin_first = np.einsum("rs,pa->rpas", eye, -np.sin(first))
    first = np.stack([cos_first, sin_first]).reshape(2 * cycle_count * outer, outer * cycle_count)
    twist = 2.0 * np.pi * np.outer(a, b) / samples
    twist = np.stack([np.tile(np.cos(twist), (cycle_count, 1)), np.tile(np.sin(twist), (cycle_count, 1))])
    last = 2.0 * np.pi * (np.outer(b, q) % LANES) / LANES
    cos_last, sin_last = np.cos(last), np.sin(last)
    last = np.block([[cos_last, -sin_last], [sin_last, cos_last]]) / math.sqrt(samples)

    def halves(table):
        table = table.astype(np.float32)
        upper = table.astype(jnp.bfloat16)
        return np.stack([upper, (table - upper.astype(np.float32)).astype(jnp.bfloat16)])

    return halves(first), twist.astype(np.float32), halves(last)


def spectrum_body(ids_ref, sky_ref, first_ref, twist_ref, last_ref, out_ref, rows_ref):
    maps_count = sky_ref.shape[0]
    owners, groups, cycle_count, lines, slots = out_ref.shape
    rows = first_ref.shape[1] // 2
    outer = rows // cycle_count
    high = last_ref.shape[2] // 2
    orders = outer * high
    first = (first_ref[0], first_ref[1])
    last = (last_ref[0], last_ref[1])
    cos_twist = twist_ref[0]
    sin_twist = twist_ref[1]

    def one_map(m, carry):
        inner = three_pass(first, split(sky_ref[m]))
        re = inner[:rows]
        im = inner[rows:]
        turned = jnp.concatenate(
            [re * cos_twist + im * sin_twist, im * cos_twist - re * sin_twist], axis=1
        )
        done = three_pass(split(turned), last)
        start = pl.multiple_of(m * 2 * high, 2 * high)
        rows_ref[pl.ds(start, 2 * high), :] = done.T
        return carry

    lax.fori_loop(0, maps_count, one_map, 0, unroll=4)

    per = 256 // outer
    total = None
    for block in range(orders // 256):
        parts = [
            rows_ref[pl.ds(block * per + i, maps_count * 2, stride=high), :] for i in range(per)
        ]
        left = jnp.concatenate(
            [
                jnp.concatenate([part[:, r * outer : (r + 1) * outer] for part in parts], axis=1)
                for r in range(cycle_count)
            ],
            axis=0,
        ).astype(BF16)
        order = block * 256 + lax.broadcasted_iota(jnp.int32, (256, orders), 0)
        pick = jnp.where(order == ids_ref[...], 1.0, 0.0).astype(BF16)
        term = jnp.dot(left, pick, preferred_element_type=F32)
        total = term if total is None else total + term
    for k in range(owners):
        picked = [
            total[r * 2 * maps_count + k * lines : r * 2 * maps_count + (k + 1) * lines]
            for r in range(cycle_count)
        ]
        both = jnp.concatenate(picked, axis=0).astype(BF16)
        for g in range(groups):
            tile = both[:, g * slots : (g + 1) * slots]
            out_ref[k, g] = tile.reshape(cycle_count, lines, slots)


def make_spectrum(sky_maps, order_of_slot, owners, groups):
    maps_count, cycle_count, samples = sky_maps.shape
    orders = order_of_slot.shape[0]
    slots = orders // groups
    first, twist, last = fourier_tables(samples, orders, cycle_count)
    outer = samples // LANES
    sky = sky_maps.reshape(maps_count, cycle_count, outer, LANES).transpose(0, 2, 1, 3)
    sky = sky.reshape(maps_count, outer * cycle_count, LANES)
    high = orders // outer
    return pl.pallas_call(
        spectrum_body,
        out_shape=jax.ShapeDtypeStruct(
            (owners, groups, cycle_count, maps_count * 2 // owners, slots), BF16
        ),
        scratch_shapes=[pltpu.VMEM((maps_count * 2 * high, LANES), F32)],
        compiler_params=pltpu.CompilerParams(vmem_limit_bytes=48 << 20),
        name="spectrum",
    )(order_of_slot.reshape(1, orders), sky, jnp.asarray(first), jnp.asarray(twist), jnp.asarray(last))


def table_body(base_ref, ids_ref, kern_ref, wig_ref, out_ref, wide_ref):
    rows, degs, slots = wig_ref.shape

    @pl.when(pl.program_id(0) == 0)
    def _():
        columns = kern_ref[...].T
        for i in range(wide_ref.shape[0]):
            wide_ref[i] = jnp.broadcast_to(columns[:, i : i + 1], (degs, slots)).astype(BF16)

    degree = base_ref[0] + lax.broadcasted_iota(jnp.int32, (slots, degs), 1)
    live = degree >= ids_ref[...]

    def turned(row):
        flat = wig_ref[row].astype(F32).T
        return jnp.where(live, flat, 0.0).reshape(slots // 8, 8, degs)

    for row in range(0, rows, 2):
        pair = jnp.concatenate([turned(row), turned(row + 1)], axis=1)
        out_ref[:, row // 2] = pair.astype(BF16)


def make_table(wigner_d, my_orders, base, kern, step):
    cycles, degs, slots = wigner_d.shape
    count = kern.shape[0]
    return pl.pallas_call(
        table_body,
        grid_spec=pltpu.PrefetchScalarGridSpec(
            num_scalar_prefetch=1,
            grid=(cycles // step,),
            in_specs=[
                pl.BlockSpec((slots, 1), lambda i, base: (0, 0)),
                pl.BlockSpec((count, degs), lambda i, base: (0, 0)),
                pl.BlockSpec((step, degs, slots), lambda i, base: (i, 0, 0)),
            ],
            out_specs=[
                pl.BlockSpec((slots // 8, step // 2, 16, degs), lambda i, base: (0, i, 0, 0)),
                pl.BlockSpec((count, degs, slots), lambda i, base: (0, 0, 0)),
            ],
        ),
        out_shape=[
            jax.ShapeDtypeStruct((slots // 8, cycles // 2, 16, degs), BF16),
            jax.ShapeDtypeStruct((count, degs, slots), BF16),
        ],
        compiler_params=pltpu.CompilerParams(vmem_limit_bytes=40 << 20),
        cost_estimate=pl.CostEstimate(
            flops=cycles * degs * slots * 16, bytes_accessed=cycles * degs * slots * 4, transcendentals=0
        ),
        name="table",
    )(base, my_orders.reshape(slots, 1), kern, wigner_d)


def combine_body(pieces, has_base, where_ref, *refs):
    parts = refs[:pieces]
    rest = refs[pieces + has_base :]
    tab_hbm, wide_hbm, out_ref, xs, dp, ht, ab, wide_ref, tab_ref, sem = rest
    cycles, per, slots = parts[0].shape
    lines = per * pieces
    groups = slots // 8
    degs = tab_ref.shape[3]
    depth = cycles * 8
    count = out_ref.shape[0]
    halves = slots // 128
    m = pl.program_id(0)
    chunks = sem.shape[0] - 1
    span = groups // chunks

    def fetch(i):
        part = pl.ds(i * span, span)
        return pltpu.make_async_copy(tab_hbm.at[part], tab_ref.at[part], sem.at[i])

    fetch_wide = pltpu.make_async_copy(wide_hbm, wide_ref, sem.at[chunks])

    @pl.when(m == 0)
    def _():
        for i in range(chunks):
            fetch(i).start()
        fetch_wide.start()
        for d in range(pieces):
            for h in range(halves):
                block = parts[d][:, :, h * 128 : (h + 1) * 128].astype(F32)
                xs[d, h] = block.reshape(cycles * per, 128)
        spread = (
            lax.broadcasted_iota(jnp.int32, (cycles, depth), 0)
            == lax.broadcasted_iota(jnp.int32, (cycles, depth), 1) // 8
        ).astype(BF16)
        keep = (lax.broadcasted_iota(jnp.int32, (128, depth), 0) % 8) == (
            lax.broadcasted_iota(jnp.int32, (128, depth), 1) % 8
        )

        def place(i, carry):
            d = i // (per // 2)
            inside = 2 * (i % (per // 2))
            for h in range(halves):
                pair = []
                for t in range(2):
                    x = xs[d, h, pl.ds(inside + t, cycles, stride=per), :].astype(BF16)
                    f = lax.dot_general(
                        x, spread, (((0,), (0,)), ((), ())), preferred_element_type=F32
                    )
                    pair.append(jnp.where(keep, f, 0.0).reshape(16, 8, depth))
                dp[h * 16 : (h + 1) * 16, i] = jnp.concatenate(pair, axis=1).astype(BF16)
            return carry

        lax.fori_loop(0, lines // 2, place, 0, unroll=PLACE_UNROLL)

        def multiply(g, carry):
            product = jnp.dot(
                dp[g].reshape(lines * 8, depth),
                tab_ref[g].reshape(depth, degs),
                preferred_element_type=F32,
            )
            ht[:, pl.ds(pl.multiple_of(g * 8, 8), 8), :] = product.reshape(lines, 8, degs)
            return carry

        for i in range(chunks):
            fetch(i).wait()
            lax.fori_loop(i * span, (i + 1) * span, multiply, 0, unroll=MULT_UNROLL)
        fetch_wide.wait()

    for c in range(2):
        turned = [ht[2 * m + c, h * 128 : (h + 1) * 128, :].T for h in range(halves)]
        ab[c] = jnp.concatenate(turned, axis=1).astype(BF16)
    for top in range(0, degs, 16):
        js = slice(top, top + 16)
        a = ab[0, js, :]
        b = ab[1, js, :]
        for n in range(count):
            p = wide_ref[2 * n, js, :]
            q = wide_ref[2 * n + 1, js, :]
            out_ref[n, 0, 0, js, :] = (a * p + b * q).astype(BF16)
            out_ref[n, 0, 1, js, :] = (b * p - a * q).astype(BF16)


def combine(parts, table, wide, where, base, maps_count):
    cycles, per, slots = parts[0].shape
    lines = per * len(parts)
    degs = table.shape[3]
    count = wide.shape[0] // 2
    once = pl.BlockSpec(
        parts[0].shape, lambda m, where: (0, 0, 0), pipeline_mode=pl.Buffered(1)
    )
    outside = pl.BlockSpec(memory_space=pl.ANY)
    has_base = int(base is not None)
    return pl.pallas_call(
        functools.partial(combine_body, len(parts), has_base),
        grid_spec=pltpu.PrefetchScalarGridSpec(
            num_scalar_prefetch=1,
            grid=(lines // 2,),
            in_specs=[once] * len(parts) + [outside] * (2 + has_base),
            out_specs=pl.BlockSpec(
                (count, 1, 2, degs, slots), lambda m, where: (0, where[m], 0, 0, 0)
            ),
            scratch_shapes=[
                pltpu.VMEM((len(parts), slots // 128, cycles * per, 128), F32),
                pltpu.VMEM((slots // 8, lines // 2, 16, cycles * 8), BF16),
                pltpu.VMEM((lines, slots, degs), F32),
                pltpu.VMEM((2, degs, slots), BF16),
                pltpu.VMEM(wide.shape, BF16),
                pltpu.VMEM(table.shape, BF16),
                pltpu.SemaphoreType.DMA((5,)),
            ],
        ),
        out_shape=jax.ShapeDtypeStruct((count, maps_count, 2, degs, slots), BF16),
        input_output_aliases={1 + len(parts): 0} if has_base else {},
        compiler_params=pltpu.CompilerParams(vmem_limit_bytes=60 << 20),
        name="combine",
    )(where, *parts, *([base] if has_base else []), table, wide)


def local(sky_maps, wigner_d, order_of_slot, kernel):
    cycles, deg_count, slot_count = wigner_d.shape
    maps_count, cycle_count, _ = sky_maps.shape
    groups = lax.axis_size("order")
    owners = lax.axis_size("blk")
    me = lax.axis_index("blk")
    my_orders = lax.dynamic_slice_in_dim(
        order_of_slot, lax.axis_index("order") * slot_count, slot_count, 0
    )
    by_owner = make_spectrum(sky_maps, order_of_slot, owners, groups)
    per = maps_count * 2 // owners
    by_owner = by_owner.reshape(owners * groups, cycle_count * per, slot_count)
    mine = lax.all_to_all(by_owner, ("blk", "order"), split_axis=0, concat_axis=0, tiled=True)
    base = (DEG_LO + me * deg_count).astype(jnp.int32).reshape(1)
    table, wide = make_table(wigner_d, my_orders, base, kernel.reshape(-1, deg_count), 8)
    mine, table, wide = lax.optimization_barrier((mine, table, wide))
    mine = mine.reshape(cycles, per, slot_count)

    def swap(part, bit):
        return lax.ppermute(part, "blk", [(i, i ^ bit) for i in range(owners)])

    far = [(0, mine)]
    bit = owners // 2
    while bit > 1:
        far = far + [(mask ^ bit, swap(part, bit)) for mask, part in far]
        bit //= 2
    pieces = []
    for mask, part in far:
        pieces += [(mask, part), (mask ^ 1, swap(part, 1))]

    def places(chosen):
        first = jnp.asarray([mask for mask, _ in chosen], dtype=jnp.int32) ^ me
        return (first[:, None] * (per // 2) + jnp.arange(per // 2, dtype=jnp.int32)).reshape(-1)

    result = None
    for chosen in (pieces[:2], pieces[2:]):
        parts = [part for _, part in chosen]
        result = combine(parts, table, wide, places(chosen), result, maps_count)
    return result


def solution(mesh):
    return jax.shard_map(
        local,
        mesh=mesh,
        in_specs=(
            P(None, ("blk", "order"), None),
            P(None, "blk", "order"),
            P(),
            P(None, None, "blk"),
        ),
        out_specs=P(None, None, None, "blk", "order"),
        check_vma=False,
    )
```

time: 92.5 us -> 85 us (0.919)
  blocking collectives: 16 us -> 0 us
  matrix products: 14.8 us -> 0 us
  Pallas kernels: 47.1 us -> 57.8 us
  starting transfers between devices: 1.52 us -> 9.07 us
  local copies, waits for them, and re-layouts: 7.35 us -> 10.6 us
  waiting for transfers between devices: 4.86 us -> 6.69 us
    all_to_all x1 -> x0, blocking collectives: 16 us -> none  [local(): lax.all_to_all(by_owner, 'order', split_axis=0, concat_axis=0, tiled=True)]
    dot_general x7 -> x0, matrix products: 14.8 us -> none  [the longest x1 5.08 us: cycle_spectrum(): jnp.einsum('abkj,km->abjm', values, jnp.sin(inner_angle), precision=HIGHEST)]
    pallas_call x1 -> x3, Pallas kernels: 32.6 us -> 43.9 us  [the longest x2 38.2 us: combine(): pl.pallas_call(functools.partial(combine_body, len(parts), has_base), gri...]
    all_to_all x0 -> x1, starting transfers between devices: none -> 7.3 us  [local(): lax.all_to_all(by_owner, ('blk', 'order'), split_axis=0, concat_axis=0, t...]
    unnamed x18 -> x22, local copies, waits for them, and re-layouts: 3.77 us -> 7.72 us
    ppermute x3, waiting for transfers between devices: 4.86 us -> 6.68 us  [swap(): return lax.ppermute(part, 'blk', [(i, i ^ bit) for i in range(owners)])]
    reshape x3 -> x1, local copies, waits for them, and re-layouts: 2.42 us -> 0.75 us  [local(): kernel.reshape(-1, deg_count)]
    add x1 -> x2, local copies, waits for them, and re-layouts: 0.09 us -> 1.25 us  [places(): first[:, None] * (per // 2) + jnp.arange(per // 2, dtype=jnp.int32)]
  transfers between devices with their start and end apart: 3 -> 4, of which waited for: 1 -> 1; matrix products, arithmetic and copies ran while one was open for 0% -> 4% of each run, Pallas kernels for 16% -> 39%
where the time goes in v2:
time: 85 us; the launch traced here: 84.4 us
  Pallas kernels  57.8 us (68%)
  local copies, waits for them, and re-layouts  10.6 us (12%)
  starting transfers between devices  9.07 us (11%)
  waiting for transfers between devices  6.69 us (8%)
    pallas_call x2, Pallas kernels, combine(): pl.pallas_call(functools.partial(combine_body, len(parts), has_base), gri...  38.2 us
    pallas_call x1, Pallas kernels, make_table(): pl.pallas_call(table_body, grid_spec=pltpu.PrefetchScalarGridSpec(num_sca...  13.9 us
    unnamed x22, local copies, waits for them, and re-layouts  7.72 us
    all_to_all x1, starting transfers between devices, local(): lax.all_to_all(by_owner, ('blk', 'order'), split_axis=0, concat_axis=0, t...  7.3 us
    ppermute x3, waiting for transfers between devices, swap(): return lax.ppermute(part, 'blk', [(i, i ^ bit) for i in range(owners)])  6.68 us
    pallas_call x1, Pallas kernels, make_spectrum(): pl.pallas_call(spectrum_body, out_shape=jax.ShapeDtypeStruct((owners, gro...  5.68 us
    ppermute x3, starting transfers between devices, swap(): return lax.ppermute(part, 'blk', [(i, i ^ bit) for i in range(owners)])  1.77 us
  transfers between devices with their start and end apart: 4, of which 1 were waited for; matrix products, arithmetic and copies ran while one was open for 4% of the time, Pallas kernels for 39%

profile of v2, /device:TPU:0, one launch (start us, length us, event | category | flops | bytes accessed | tf_op | source)
XLA Modules:
  0.0 84.4 jit_solution(17403919029415304173)
XLA Ops:
  0.0 0.0 copy-start.10
  0.0 0.0 copy-start.1
  0.0 1.2 %copy-done.1 = f32[16,2,8192]{2,1,0:T(2,128)S(1)} copy-done((f32[16,2,8192]{2,1,0:T(2,128)S(1)}, f32[16,2,8192]{2,1,0:T(2,128)}, u32[]{:S(2)}) %copy-start.1) | copy-done | bytes 1048600
  1.2 0.0 copy-start.2
  1.2 0.9 %copy-done.2 = bf16[2,256,64]{2,1,0:T(8,128)(2,1)S(1)} copy-done((bf16[2,256,64]{2,1,0:T(8,128)(2,1)S(1)}, bf16[2,256,64]{2,1,0:T(8,128)(2,1)}, u32[]{:S(2)}) %copy-start.2) | copy-done | bytes 65560
  2.1 0.0 copy-start.3
  2.1 0.9 %copy-done.3 = f32[2,128,128]{2,1,0:T(8,128)S(1)} copy-done((f32[2,128,128]{2,1,0:T(8,128)S(1)}, f32[2,128,128]{2,1,0:T(8,128)}, u32[]{:S(2)}) %copy-start.3) | copy-done | bytes 131096
  3.1 0.0 copy-start.4
  3.1 0.9 %copy-done.4 = bf16[2,256,128]{2,1,0:T(8,128)(2,1)S(1)} copy-done((bf16[2,256,128]{2,1,0:T(8,128)(2,1)S(1)}, bf16[2,256,128]{2,1,0:T(8,128)(2,1)}, u32[]{:S(2)}) %copy-start.4) | copy-done | bytes 131096
  4.0 0.0 copy-start.5
  4.0 0.7 copy-done.5
  4.7 5.7 %spectrum.1 = bf16[4,8,2,8,256]{4,3,2,1,0:T(8,128)(2,1)} custom-call(s32[1,2048]{1,0:T(1,128)S(1)} %bitcast.11, f32[16,128,128]{2,1,0:T(8,128)S(1)} %bitcast.10, bf16[2,256,128]{2,1,0:T(8,128)(2,1)S(1)} %copy-done.4, f32[2,128,128]{2,1,0:T(8,128)S(1)} %copy-done.3, bf16[2,256,64]{2,1,0:T(8,128)(2,1)S(1)} %copy-done.2), custom_call_target="tpu_custom_call" | custom-call | tf_op jit(solution)/shard_map/spectrum/pallas_call | solution.py:119
  10.3 7.3 %all-to-all-start = ((bf16[32,16,256]{2,1,0:T(8,128)(2,1)}), bf16[32,16,256]{2,1,0:T(8,128)(2,1)S(1)}, u32[]{:S(2)}, u32[]{:S(2)}) async-start(bf16[32,16,256]{2,1,0:T(8,128)(2,1)} %bitcast.4), calls=%async_computation | async-start | bytes 524288 | tf_op jit(solution)/shard_map/all_to_all | solution.py:311
  17.7 0.8 dynamic_slice.3
  18.4 0.8 reshape.42.kern_ref
  19.2 0.1 copy.13.ids_ref
  19.3 13.9 %table.1 = (bf16[32,32,16,384]{3,2,1,0:T(8,128)(2,1)}, bf16[16,384,256]{2,1,0:T(8,128)(2,1)S(1)}) custom-call(s32[1]{0:T(128)} %bitcast.5.base_ref, s32[256,1]{1,0:T(8,128)S(1)} %copy.13.ids_ref, f32[16,384]{1,0:T(8,128)S(1)} %reshape.42.kern_ref, bf16[64,384,256]{2,1,0:T(8,128)(2,1)} %wig_ref.1), custom_call_target="tpu_custom_call" | custom-call | flops 100663296 | bytes 25165824 | tf_op jit(solution)/shard_map/table/pallas_call | solution.py:154
  33.2 0.0 copy-start
  33.2 1.7 %copy-done = bf16[16,384,256]{2,1,0:T(8,128)(2,1)} copy-done((bf16[16,384,256]{2,1,0:T(8,128)(2,1)}, bf16[16,384,256]{2,1,0:T(8,128)(2,1)S(1)}, u32[]{:S(2)}) %copy-start) | copy-done | bytes 3145752
  34.9 0.0 all-to-all-done
  34.9 0.0 copy-start.6
  34.9 1.8 %collective-permute-start = (bf16[64,8,256]{2,1,0:T(8,128)(2,1)S(1)}, bf16[64,8,256]{2,1,0:T(8,128)(2,1)S(1)}, u32[]{:S(2)}, u32[]{:S(2)}) collective-permute-start(bf16[64,8,256]{2,1,0:T(8,128)(2,1)S(1)} %bitcast.12), channel_id=1, source_target_pairs={{0,16},{8,24},{16,0},{24,8},{1,17},{9,25},{17,1},{25,9},{2,18},{10... | collective-permute-start | bytes 786440 | tf_op jit(solution)/shard_map/ppermute | solution.py:318
  36.7 0.0 copy-done.10
  36.7 0.0 collective-permute-start.2
  36.7 6.7 %collective-permute-done.refs_0_ = bf16[64,8,256]{2,1,0:T(8,128)(2,1)S(1)} collective-permute-done((bf16[64,8,256]{2,1,0:T(8,128)(2,1)S(1)}, bf16[64,8,256]{2,1,0:T(8,128)(2,1)S(1)}, u32[]{:S(2)}, u32[]{:S(2)}) %collective-permute-start) | collective-permute-done | bytes 262176 | tf_op jit(solution)/shard_map/ppermute | solution.py:318
  43.4 0.0 copy-start.7
  43.4 0.0 collective-permute-start.1
  43.4 0.1 iota_add_fusion
  43.4 0.6 add.45.where_ref
  44.1 0.1 iota_add_fusion.1
  44.1 0.6 add.40.where_ref
  44.8 0.0 collective-permute-done.2.refs_1_
  44.8 0.0 copy-done.6
  44.8 0.0 copy-start.9
  44.8 0.7 copy-done.9
  45.5 19.1 %combine.2.refs_2_ = bf16[8,16,2,384,256]{4,3,2,1,0:T(8,128)(2,1)} custom-call(s32[8]{0:T(128)} %add.45.where_ref, bf16[64,8,256]{2,1,0:T(8,128)(2,1)} %bitcast.14, bf16[64,8,256]{2,1,0:T(8,128)(2,1)} %copy-done.9, bf16[32,32,16,384]{3,2,1,0:T(8,128)(2,1)} %get-tuple-element.13.refs_2_.refs_3_, bf16[16,384,256]{2,1,0:T(8,128)(2,1)} %copy-done), custom_call_target="tpu_custom_call" | custom-call | tf_op jit(solution)/shard_map/combine/pallas_call | solution.py:273
  64.6 0.0 copy-done.7
  64.6 0.0 collective-permute-done.1.refs_1_
  64.6 0.0 copy-start.8
  64.6 0.7 copy-done.8
  65.3 19.1 %combine.3 = bf16[8,16,2,384,256]{4,3,2,1,0:T(8,128)(2,1)} custom-call(s32[8]{0:T(128)} %add.40.where_ref, bf16[64,8,256]{2,1,0:T(8,128)(2,1)} %copy-done.7, bf16[64,8,256]{2,1,0:T(8,128)(2,1)} %copy-done.8, bf16[8,16,2,384,256]{4,3,2,1,0:T(8,128)(2,1)} %combine.2.refs_2_, ...), custom_call_target="tpu_custom_call", output_to_operand_aliasing={{}: (3, {})} | custom-call | tf_op jit(solution)/shard_map/combine/pallas_call | solution.py:273
  (1 shorter events, 0.0 us)
Async XLA Ops:
  0.0 36.7 %copy-start.10 = (s32[2]{0:T(128)S(1)}, s32[2]{0:T(128)}, u32[]{:S(2)}) copy-start(s32[2]{0:T(128)} %constant.33.clone) | copy-start | bytes 28
  0.0 1.2 %copy-start.1 = (f32[16,2,8192]{2,1,0:T(2,128)S(1)}, f32[16,2,8192]{2,1,0:T(2,128)}, u32[]{:S(2)}) copy-start(f32[16,2,8192]{2,1,0:T(2,128)} %param.9) | copy-start | bytes 3145732
  1.2 0.9 %copy-start.2 = (bf16[2,256,64]{2,1,0:T(8,128)(2,1)S(1)}, bf16[2,256,64]{2,1,0:T(8,128)(2,1)}, u32[]{:S(2)}) copy-start(bf16[2,256,64]{2,1,0:T(8,128)(2,1)} %constant.32.clone.last_ref) | copy-start | bytes 196612
  2.1 0.9 %copy-start.3 = (f32[2,128,128]{2,1,0:T(8,128)S(1)}, f32[2,128,128]{2,1,0:T(8,128)}, u32[]{:S(2)}) copy-start(f32[2,128,128]{2,1,0:T(8,128)} %constant.31.clone.twist_ref) | copy-start | bytes 393220
  3.1 0.9 %copy-start.4 = (bf16[2,256,128]{2,1,0:T(8,128)(2,1)S(1)}, bf16[2,256,128]{2,1,0:T(8,128)(2,1)}, u32[]{:S(2)}) copy-start(bf16[2,256,128]{2,1,0:T(8,128)(2,1)} %constant.30.clone.first_ref) | copy-start | bytes 393220
  4.0 0.7 copy-start.5
  10.3 24.6 %all-to-all-start = ((bf16[32,16,256]{2,1,0:T(8,128)(2,1)}), bf16[32,16,256]{2,1,0:T(8,128)(2,1)S(1)}, u32[]{:S(2)}, u32[]{:S(2)}) async-start(bf16[32,16,256]{2,1,0:T(8,128)(2,1)} %bitcast.4), calls=%async_computation | async-start | bytes 524288 | tf_op jit(solution)/shard_map/all_to_all | solution.py:311
  33.2 1.7 %copy-start = (bf16[16,384,256]{2,1,0:T(8,128)(2,1)}, bf16[16,384,256]{2,1,0:T(8,128)(2,1)S(1)}, u32[]{:S(2)}) copy-start(bf16[16,384,256]{2,1,0:T(8,128)(2,1)S(1)} %get-tuple-element.14.refs_3_.refs_4_) | copy-start | bytes 9437188
  34.9 9.9 %copy-start.6 = (bf16[32,16,256]{2,1,0:T(8,128)(2,1)}, bf16[32,16,256]{2,1,0:T(8,128)(2,1)S(1)}, u32[]{:S(2)}) copy-start(bf16[32,16,256]{2,1,0:T(8,128)(2,1)S(1)} %all-to-all-done) | copy-start | bytes 786436
  34.9 8.5 %collective-permute-start = (bf16[64,8,256]{2,1,0:T(8,128)(2,1)S(1)}, bf16[64,8,256]{2,1,0:T(8,128)(2,1)S(1)}, u32[]{:S(2)}, u32[]{:S(2)}) collective-permute-start(bf16[64,8,256]{2,1,0:T(8,128)(2,1)S(1)} %bitcast.12), channel_id=1, source_target_pairs={{0,16},{8,24},{16,0},{24,8},{1,17},{9,25},{17,1},{25,9},{2,18},{10... | collective-permute-start | bytes 786440 | tf_op jit(solution)/shard_map/ppermute | solution.py:318
  36.7 8.1 %collective-permute-start.2 = (bf16[64,8,256]{2,1,0:T(8,128)(2,1)S(1)}, bf16[64,8,256]{2,1,0:T(8,128)(2,1)S(1)}, u32[]{:S(2)}, u32[]{:S(2)}) collective-permute-start(bf16[64,8,256]{2,1,0:T(8,128)(2,1)S(1)} %bitcast.13), channel_id=1, source_target_pairs={{0,8},{8,0},{16,24},{24,16},{1,9},{9,1},{17,25},{25,17},{2,10},{10... | collective-permute-start | bytes 786440 | tf_op jit(solution)/shard_map/ppermute | solution.py:318
  43.4 21.2 %copy-start.7 = (bf16[64,8,256]{2,1,0:T(8,128)(2,1)}, bf16[64,8,256]{2,1,0:T(8,128)(2,1)S(1)}, u32[]{:S(2)}) copy-start(bf16[64,8,256]{2,1,0:T(8,128)(2,1)S(1)} %collective-permute-done.refs_0_) | copy-start | bytes 786436
  43.4 21.2 %collective-permute-start.1 = (bf16[64,8,256]{2,1,0:T(8,128)(2,1)S(1)}, bf16[64,8,256]{2,1,0:T(8,128)(2,1)S(1)}, u32[]{:S(2)}, u32[]{:S(2)}) collective-permute-start(bf16[64,8,256]{2,1,0:T(8,128)(2,1)S(1)} %collective-permute-done.refs_0_), channel_id=1, source_target_pairs={{0,8},{8,0},{16,24},{24,16},{1,9},{9,1},{17,25},{25,17},{2,10},{10... | collective-permute-start | bytes 786440 | tf_op jit(solution)/shard_map/ppermute | solution.py:318
  44.8 0.7 copy-start.9
  64.6 0.7 copy-start.8

commit v3 on v2

v3 whole, which is shorter than its diff:
```python
import functools
import math

import jax
import jax.numpy as jnp
import numpy as np
from jax import lax
from jax.experimental import pallas as pl
from jax.experimental.pallas import tpu as pltpu
from jax.sharding import PartitionSpec as P

DEG_LO = 512
LANES = 128
F32 = jnp.float32
BF16 = jnp.bfloat16


def split(value):
    high = value.astype(BF16)
    return high, (value - high.astype(F32)).astype(BF16)


def three_pass(left, right):
    out = jnp.dot(left[0], right[0], preferred_element_type=F32)
    out += jnp.dot(left[0], right[1], preferred_element_type=F32)
    return out + jnp.dot(left[1], right[0], preferred_element_type=F32)


def fourier_tables(samples, orders, cycle_count):
    outer = samples // LANES
    high = orders // outer
    a = np.arange(outer)
    b = np.arange(LANES)
    q = np.arange(high)
    first = 2.0 * np.pi * (np.outer(a, a) % outer) / outer
    eye = np.eye(cycle_count)
    cos_first = np.einsum("rs,pa->rpas", eye, np.cos(first))
    sin_first = np.einsum("rs,pa->rpas", eye, -np.sin(first))
    first = np.stack([cos_first, sin_first]).reshape(2 * cycle_count * outer, outer * cycle_count)
    twist = 2.0 * np.pi * np.outer(a, b) / samples
    twist = np.stack([np.tile(np.cos(twist), (cycle_count, 1)), np.tile(np.sin(twist), (cycle_count, 1))])
    last = 2.0 * np.pi * (np.outer(b, q) % LANES) / LANES
    cos_last, sin_last = np.cos(last), np.sin(last)
    last = np.block([[cos_last, -sin_last], [sin_last, cos_last]]) / math.sqrt(samples)

    def halves(table):
        table = table.astype(np.float32)
        upper = table.astype(jnp.bfloat16)
        return np.stack([upper, (table - upper.astype(np.float32)).astype(jnp.bfloat16)])

    last = np.pad(last, ((0, 0), (0, LANES - last.shape[1] % LANES if last.shape[1] % LANES else 0)))
    tables = [halves(first), halves(twist.reshape(-1, LANES)), halves(last)]
    return np.concatenate([table.reshape(-1, LANES) for table in tables])


def spectrum_body(ids_ref, *refs):
    sky_ref, table_ref, out_ref, rows_ref = refs
    maps_count, rows, _ = sky_ref.shape
    owners, groups, cycle_count, lines, slots = out_ref.shape
    outer = rows // cycle_count
    orders = groups * slots
    high = orders // outer
    first = (table_ref[: 2 * rows], table_ref[2 * rows : 4 * rows])
    twist = table_ref[4 * rows : 6 * rows].astype(F32) + table_ref[6 * rows : 8 * rows].astype(F32)
    cos_twist = twist[:rows]
    sin_twist = twist[rows:]
    last = (table_ref[8 * rows : 8 * rows + 256, :], table_ref[8 * rows + 256 :, :])

    def one_map(m, carry):
        inner = three_pass(first, split(sky_ref[m]))
        re = inner[:rows]
        im = inner[rows:]
        turned = jnp.concatenate(
            [re * cos_twist + im * sin_twist, im * cos_twist - re * sin_twist], axis=1
        )
        done = three_pass(split(turned), last)
        start = pl.multiple_of(m * 2 * high, 2 * high)
        rows_ref[pl.ds(start, 2 * high), :] = done.T[: 2 * high]
        return carry

    lax.fori_loop(0, maps_count, one_map, 0, unroll=4)

    per = 256 // outer
    total = None
    for block in range(orders // 256):
        parts = [
            rows_ref[pl.ds(block * per + i, maps_count * 2, stride=high), :] for i in range(per)
        ]
        left = jnp.concatenate(
            [
                jnp.concatenate([part[:, r * outer : (r + 1) * outer] for part in parts], axis=1)
                for r in range(cycle_count)
            ],
            axis=0,
        ).astype(BF16)
        order = block * 256 + lax.broadcasted_iota(jnp.int32, (256, orders), 0)
        pick = jnp.where(order == ids_ref[...], 1.0, 0.0).astype(BF16)
        term = jnp.dot(left, pick, preferred_element_type=F32)
        total = term if total is None else total + term
    for k in range(owners):
        picked = [
            total[r * 2 * maps_count + k * lines : r * 2 * maps_count + (k + 1) * lines]
            for r in range(cycle_count)
        ]
        both = jnp.concatenate(picked, axis=0).astype(BF16)
        for g in range(groups):
            tile = both[:, g * slots : (g + 1) * slots]
            out_ref[k, g] = tile.reshape(cycle_count, lines, slots)


def make_spectrum(sky_maps, order_of_slot, owners, groups):
    maps_count, cycle_count, samples = sky_maps.shape
    orders = order_of_slot.shape[0]
    slots = orders // groups
    tables = fourier_tables(samples, orders, cycle_count)
    outer = samples // LANES
    sky = sky_maps.reshape(maps_count, cycle_count, outer, LANES).transpose(0, 2, 1, 3)
    sky = sky.reshape(maps_count, outer * cycle_count, LANES)
    high = orders // outer
    return pl.pallas_call(
        spectrum_body,
        out_shape=jax.ShapeDtypeStruct(
            (owners, groups, cycle_count, maps_count * 2 // owners, slots), BF16
        ),
        scratch_shapes=[pltpu.VMEM((maps_count * 2 * high, LANES), F32)],
        compiler_params=pltpu.CompilerParams(vmem_limit_bytes=20 << 20),
        name="spectrum",
    )(order_of_slot.reshape(1, orders), sky, jnp.asarray(tables))


def table_body(info_ref, ids_ref, wig_hbm, out_hbm, wig_ref, out_ref, in_sem, out_sem):
    rows, degs, slots = wig_ref.shape
    chunks = in_sem.shape[0]
    step = rows // chunks

    def fetch(i):
        part = pl.ds(i * step, step)
        return pltpu.make_async_copy(wig_hbm.at[part], wig_ref.at[part], in_sem.at[i])

    def flush(i):
        part = pl.ds(i * (step // 2), step // 2)
        return pltpu.make_async_copy(out_ref.at[:, part], out_hbm.at[:, part], out_sem.at[i])

    for i in range(chunks):
        fetch(i).start()
    start = pl.multiple_of(info_ref[1] * slots, LANES)
    ids = ids_ref[:, pl.ds(start, slots)]
    degree = DEG_LO + info_ref[0] * degs + lax.broadcasted_iota(jnp.int32, (degs, slots), 0)
    live = degree >= ids

    def turned(row):
        flat = jnp.where(live, wig_ref[row].astype(F32), 0.0)
        return flat.T.reshape(slots // 8, 8, degs)

    def one(i):
        fetch(i).wait()
        for row in range(0, step, 2):
            both = [turned(i * step + row), turned(i * step + row + 1)]
            out_ref[:, i * (step // 2) + row // 2] = jnp.concatenate(both, axis=1).astype(BF16)
        flush(i).start()

    loop(chunks, 2, one)
    for i in range(chunks):
        flush(i).wait()


def make_table(info, wigner_d, order_of_slot):
    cycles, degs, slots = wigner_d.shape
    outside = pl.BlockSpec(memory_space=pl.ANY)
    shape = (slots // 8, cycles // 2, 16, degs)
    return pl.pallas_call(
        table_body,
        in_specs=[
            pl.BlockSpec(memory_space=pltpu.SMEM),
            pl.BlockSpec(memory_space=pltpu.VMEM),
            outside,
        ],
        out_specs=outside,
        out_shape=jax.ShapeDtypeStruct(shape, BF16),
        scratch_shapes=[
            pltpu.VMEM(wigner_d.shape, BF16),
            pltpu.VMEM(shape, BF16),
            pltpu.SemaphoreType.DMA((16,)),
            pltpu.SemaphoreType.DMA((16,)),
        ],
        compiler_params=pltpu.CompilerParams(vmem_limit_bytes=58 << 20),
        cost_estimate=pl.CostEstimate(
            flops=cycles * degs * slots * 16, bytes_accessed=cycles * degs * slots * 4, transcendentals=0
        ),
        name="table",
    )(info, order_of_slot.reshape(1, -1), wigner_d)


def stage(parts, xs):
    cycles, per, slots = parts[0].shape
    for d, part in enumerate(parts):
        for h in range(slots // LANES):
            block = part[:, :, h * LANES : (h + 1) * LANES].astype(F32)
            xs[d, h] = block.reshape(cycles * per, LANES)


def place(pair, per, xs, dp):
    depth = dp.shape[3]
    cycles = depth // 8
    spread = (
        lax.broadcasted_iota(jnp.int32, (cycles, depth), 0)
        == lax.broadcasted_iota(jnp.int32, (cycles, depth), 1) // 8
    ).astype(BF16)
    keep = (lax.broadcasted_iota(jnp.int32, (LANES, depth), 0) % 8) == (
        lax.broadcasted_iota(jnp.int32, (LANES, depth), 1) % 8
    )
    d = pair // (per // 2)
    inside = 2 * (pair % (per // 2))
    for h in range(xs.shape[1]):
        both = []
        for t in range(2):
            x = xs[d, h, pl.ds(inside + t, cycles, stride=per), :].astype(BF16)
            f = lax.dot_general(x, spread, (((0,), (0,)), ((), ())), preferred_element_type=F32)
            both.append(jnp.where(keep, f, 0.0).reshape(16, 8, depth))
        dp[h * 16 : (h + 1) * 16, pair] = jnp.concatenate(both, axis=1).astype(BF16)


def multiply(g, dp, tab_ref, ht):
    lines = ht.shape[0]
    depth, degs = dp.shape[3], tab_ref.shape[3]
    product = jnp.dot(
        dp[g].reshape(lines * 8, depth),
        tab_ref[g].reshape(depth, degs),
        preferred_element_type=F32,
    )
    ht[:, pl.ds(pl.multiple_of(g * 8, 8), 8), :] = product.reshape(lines, 8, degs)


def turn(ht, line):
    halves = ht.shape[1] // LANES
    turned = [ht[line, h * LANES : (h + 1) * LANES, :].T for h in range(halves)]
    return jnp.concatenate(turned, axis=1).astype(BF16)


def loop(count, unroll, body):
    def one(i, carry):
        body(i)
        return carry

    lax.fori_loop(0, count, one, 0, unroll=min(unroll, count))


def products_body(pieces, kern_ref, *refs):
    parts = refs[:pieces]
    tab_hbm, out_ref, wide_ref, xs, dp, ht, tab_ref, sem = refs[pieces:]
    per = parts[0].shape[1]
    lines, degs, slots = out_ref.shape
    chunks = sem.shape[0]
    span = tab_ref.shape[0] // chunks

    def fetch(i):
        part = pl.ds(i * span, span)
        return pltpu.make_async_copy(tab_hbm.at[part], tab_ref.at[part], sem.at[i])

    for i in range(chunks):
        fetch(i).start()
    stage(parts, xs)
    loop(lines // 2, 8, lambda i: place(i, per, xs, dp))
    columns = jnp.concatenate([kern_ref[n] for n in range(kern_ref.shape[0])], axis=0).T
    for i in range(wide_ref.shape[0]):
        wide_ref[i] = jnp.broadcast_to(columns[:, i : i + 1], (degs, slots)).astype(BF16)
    for i in range(chunks):
        fetch(i).wait()
        loop(span, 4, lambda g: multiply(i * span + g, dp, tab_ref, ht))

    def put(line):
        out_ref[line] = turn(ht, line)

    loop(lines, 4, put)


def scratch(pieces, cycles, per, slots, degs):
    lines = pieces * per
    return [
        pltpu.VMEM((pieces, slots // LANES, cycles * per, LANES), F32),
        pltpu.VMEM((slots // 8, lines // 2, 16, cycles * 8), BF16),
        pltpu.VMEM((lines, slots, degs), F32),
    ]


def products(parts, table, kernel):
    cycles, per, slots = parts[0].shape
    degs = table.shape[3]
    lines = per * len(parts)
    whole = pl.BlockSpec(memory_space=pltpu.VMEM)
    return pl.pallas_call(
        functools.partial(products_body, len(parts)),
        in_specs=[whole] * (len(parts) + 1) + [pl.BlockSpec(memory_space=pl.ANY)],
        out_specs=[whole, whole],
        out_shape=[
            jax.ShapeDtypeStruct((lines, degs, slots), BF16),
            jax.ShapeDtypeStruct((kernel.shape[0] * 2, degs, slots), BF16),
        ],
        scratch_shapes=scratch(len(parts), cycles, per, slots, degs)
        + [pltpu.VMEM(table.shape, BF16), pltpu.SemaphoreType.DMA((8,))],
        compiler_params=pltpu.CompilerParams(vmem_limit_bytes=40 << 20),
        cost_estimate=pl.CostEstimate(
            flops=2 * lines * 8 * cycles * slots * degs, bytes_accessed=20 << 20, transcendentals=0
        ),
        name="products",
    )(kernel, *parts, table)


def combine_body(pieces, ready, info_ref, *refs):
    parts = refs[:pieces]
    held_ref, tab_hbm, wide_ref, out_ref, xs, dp, ht, ab, tab_ref, sem = refs[pieces:]
    per = parts[0].shape[1]
    groups, pairs = dp.shape[:2]
    degs = tab_ref.shape[3]
    count = out_ref.shape[0]
    m = pl.program_id(0)
    early = 2 if ready >= 4 else 1
    late = max(ready - early, 1)
    each = pl.cdiv(pairs, early)
    some = pl.cdiv(groups, late)

    fetch = pltpu.make_async_copy(tab_hbm, tab_ref, sem.at[0])

    @pl.when(m == 0)
    def _():
        fetch.start()
        stage(parts, xs)

    @pl.when(m == early)
    def _():
        fetch.wait()

    @pl.when(m < early)
    def _():
        loop(each, 8, lambda i: place(jnp.minimum(m * each + i, pairs - 1), per, xs, dp))

    @pl.when((m >= early) & (m < early + late))
    def _():
        def one(i):
            multiply(jnp.minimum((m - early) * some + i, groups - 1), dp, tab_ref, ht)

        loop(some, 6, one)

    @pl.when(m < ready)
    def _():
        ab[...] = held_ref[...]

    @pl.when(m >= ready)
    def _():
        for c in range(2):
            ab[c] = turn(ht, 2 * (m - ready) + c)

    for top in range(0, degs, 16):
        js = slice(top, top + 16)
        a = ab[0, js, :]
        b = ab[1, js, :]
        for n in range(count):
            p = wide_ref[2 * n, js, :]
            q = wide_ref[2 * n + 1, js, :]
            out_ref[n, 0, 0, js, :] = (a * p + b * q).astype(BF16)
            out_ref[n, 0, 1, js, :] = (b * p - a * q).astype(BF16)


def combine(info, parts, held, table, wide, owners):
    cycles, per, slots = parts[0].shape
    degs = table.shape[3]
    count = wide.shape[0] // 2
    ready = held.shape[0] // 2
    maps_count = ready + per * len(parts) // 2
    each = per // 2

    def out_index(m, info):
        piece = m // each
        mask = piece & 1
        far = piece >> 1
        bit = owners // 2
        while bit > 1:
            mask = mask + (far & 1) * bit
            far = far >> 1
            bit //= 2
        return (0, (mask ^ info[0]) * each + m % each, 0, 0, 0)

    whole = pl.BlockSpec(memory_space=pltpu.VMEM)
    return pl.pallas_call(
        functools.partial(combine_body, len(parts), ready),
        grid_spec=pltpu.PrefetchScalarGridSpec(
            num_scalar_prefetch=1,
            grid=(maps_count,),
            in_specs=[whole] * len(parts)
            + [
                pl.BlockSpec(
                    (2, degs, slots), lambda m, info: (jnp.minimum(m, ready - 1), 0, 0)
                ),
                pl.BlockSpec(memory_space=pl.ANY),
                whole,
            ],
            out_specs=pl.BlockSpec((count, 1, 2, degs, slots), out_index),
            scratch_shapes=scratch(len(parts), cycles, per, slots, degs)
            + [
                pltpu.VMEM((2, degs, slots), BF16),
                pltpu.VMEM(table.shape, BF16),
                pltpu.SemaphoreType.DMA((1,)),
            ],
        ),
        out_shape=jax.ShapeDtypeStruct((count, maps_count, 2, degs, slots), BF16),
        compiler_params=pltpu.CompilerParams(vmem_limit_bytes=40 << 20),
        name="combine",
    )(info, *parts, held, table, wide)


def local(sky_maps, wigner_d, order_of_slot, kernel):
    cycles, deg_count, slot_count = wigner_d.shape
    maps_count, cycle_count, _ = sky_maps.shape
    groups = lax.axis_size("order")
    owners = lax.axis_size("blk")
    info = jnp.stack([lax.axis_index("blk"), lax.axis_index("order")]).astype(jnp.int32)
    by_owner = make_spectrum(sky_maps, order_of_slot, owners, groups)
    per = maps_count * 2 // owners
    by_owner = by_owner.reshape(owners * groups, cycle_count * per, slot_count)
    mine = lax.all_to_all(by_owner, ("blk", "order"), split_axis=0, concat_axis=0, tiled=True)
    table = make_table(info, wigner_d, order_of_slot)
    mine, table = lax.optimization_barrier((mine, table))
    mine = mine.reshape(cycles, per, slot_count)

    def swap(part, bit):
        return lax.ppermute(part, "blk", [(i, i ^ bit) for i in range(owners)])

    far = [mine]
    bit = owners // 2
    while bit > 1:
        far = far + [swap(part, bit) for part in far]
        bit //= 2
    held, wide = products([mine, swap(mine, 1)], table, kernel)
    held, *far = lax.optimization_barrier((held, *far[1:]))
    parts = []
    for part in far:
        parts += [part, swap(part, 1)]
    return combine(info, parts, held, table, wide, owners)


def solution(mesh):
    return jax.shard_map(
        local,
        mesh=mesh,
        in_specs=(
            P(None, ("blk", "order"), None),
            P(None, "blk", "order"),
            P(),
            P(None, None, "blk"),
        ),
        out_specs=P(None, None, None, "blk", "order"),
        check_vma=False,
    )
```

time: 85 us -> 63.3 us (0.74)
  Pallas kernels: 57.8 us -> 48.4 us
  local copies, waits for them, and re-layouts: 10.6 us -> 2.92 us
  waiting for transfers between devices: 6.69 us -> 1.48 us
    pallas_call x3, Pallas kernels: 52.1 us -> 42.7 us  [the longest x1 25.1 us: combine(): pl.pallas_call(functools.partial(combine_body, len(parts), ready), grid_s...]
    ppermute x3, waiting for transfers between devices: 6.68 us -> 1.48 us  [swap(): return lax.ppermute(part, 'blk', [(i, i ^ bit) for i in range(owners)])]
    unnamed x22 -> x10, local copies, waits for them, and re-layouts: 7.72 us -> 2.92 us
    add x2 -> x0, local copies, waits for them, and re-layouts: 1.25 us -> none  [places(): first[:, None] * (per // 2) + jnp.arange(per // 2, dtype=jnp.int32)]
    reshape x2 -> x0, local copies, waits for them, and re-layouts: 0.89 us -> none  [the longest x1 0.75 us: local(): kernel.reshape(-1, deg_count)]
  transfers between devices with their start and end apart: 4 -> 4, of which waited for: 1 -> 1; matrix products, arithmetic and copies ran while one was open for 4% -> 1% of each run, Pallas kernels for 39% -> 28%
where the time goes in v3:
time: 63.3 us; the launch traced here: 62.9 us
  Pallas kernels  48.4 us (76%)
  starting transfers between devices  9.43 us (15%)
  local copies, waits for them, and re-layouts  2.92 us (5%)
  waiting for transfers between devices  1.48 us (2%)
    pallas_call x1, Pallas kernels, combine(): pl.pallas_call(functools.partial(combine_body, len(parts), ready), grid_s...  25.1 us
    pallas_call x1, Pallas kernels, make_table(): pl.pallas_call(table_body, in_specs=[pl.BlockSpec(memory_space=pltpu.SMEM...  10.4 us
    all_to_all x1, starting transfers between devices, local(): lax.all_to_all(by_owner, ('blk', 'order'), split_axis=0, concat_axis=0, t...  7.3 us
    pallas_call x1, Pallas kernels, products(): pl.pallas_call(functools.partial(products_body, len(parts)), in_specs=[wh...  7.23 us
    pallas_call x1, Pallas kernels, make_spectrum(): pl.pallas_call(spectrum_body, out_shape=jax.ShapeDtypeStruct((owners, gro...  5.7 us
    unnamed x10, local copies, waits for them, and re-layouts  2.92 us
    ppermute x3, starting transfers between devices, swap(): return lax.ppermute(part, 'blk', [(i, i ^ bit) for i in range(owners)])  2.13 us
    ppermute x3, waiting for transfers between devices, swap(): return lax.ppermute(part, 'blk', [(i, i ^ bit) for i in range(owners)])  1.48 us
  transfers between devices with their start and end apart: 4, of which 1 were waited for; matrix products, arithmetic and copies ran while one was open for 1% of the time, Pallas kernels for 28%

profile of v3, /device:TPU:0, one launch (start us, length us, event | category | flops | bytes accessed | tf_op | source)
XLA Modules:
  0.0 62.9 jit_solution(18098881672546778668)
XLA Ops:
  0.0 0.0 copy-start
  0.0 1.2 %copy-done = f32[16,2,8192]{2,1,0:T(2,128)S(1)} copy-done((f32[16,2,8192]{2,1,0:T(2,128)S(1)}, f32[16,2,8192]{2,1,0:T(2,128)}, u32[]{:S(2)}) %copy-start) | copy-done | bytes 1048600
  1.2 0.0 copy-start.1
  1.2 1.0 %copy-done.1 = bf16[1536,128]{1,0:T(8,128)(2,1)S(1)} copy-done((bf16[1536,128]{1,0:T(8,128)(2,1)S(1)}, bf16[1536,128]{1,0:T(8,128)(2,1)}, u32[]{:S(2)}) %copy-start.1) | copy-done | bytes 393240
  2.2 0.0 copy-start.2
  2.2 0.7 %copy-done.2 = s32[2048]{0:T(1024)S(1)} copy-done((s32[2048]{0:T(1024)S(1)}, s32[2048]{0:T(1024)}, u32[]{:S(2)}) %copy-start.2) | copy-done | bytes 8216
  2.9 5.7 %spectrum.1 = bf16[4,8,2,8,256]{4,3,2,1,0:T(8,128)(2,1)} custom-call(s32[1,2048]{1,0:T(1,128)S(1)} %bitcast.15, f32[16,128,128]{2,1,0:T(8,128)S(1)} %bitcast.13, bf16[1536,128]{1,0:T(8,128)(2,1)S(1)} %copy-done.1), custom_call_target="tpu_custom_call" | custom-call | tf_op jit(solution)/shard_map/spectrum/pallas_call | solution.py:120
  8.6 7.3 %all-to-all-start = ((bf16[32,16,256]{2,1,0:T(8,128)(2,1)}), bf16[32,16,256]{2,1,0:T(8,128)(2,1)S(1)}, u32[]{:S(2)}, u32[]{:S(2)}) async-start(bf16[32,16,256]{2,1,0:T(8,128)(2,1)} %bitcast.6), calls=%async_computation | async-start | bytes 524288 | tf_op jit(solution)/shard_map/all_to_all | solution.py:420
  15.9 0.6 pad_add_fusion.info_ref
  16.5 0.0 copy-start.3
  16.5 10.4 %table.1.refs_2_.refs_3_ = bf16[32,32,16,384]{3,2,1,0:T(8,128)(2,1)} custom-call(s32[2]{0:T(128)} %pad_add_fusion.info_ref, s32[1,2048]{1,0:T(1,128)} %bitcast.14, bf16[64,384,256]{2,1,0:T(8,128)(2,1)} %wig_hbm.1), custom_call_target="tpu_custom_call" | custom-call | flops 100663296 | bytes 25165824 | tf_op jit(solution)/shard_map/table/pallas_call | solution.py:171
  26.9 0.0 copy-start.4
  26.9 0.0 all-to-all-done
  27.0 0.3 collective-permute-start
  27.3 1.7 %collective-permute-start.1 = (bf16[64,8,256]{2,1,0:T(8,128)(2,1)S(1)}, bf16[64,8,256]{2,1,0:T(8,128)(2,1)S(1)}, u32[]{:S(2)}, u32[]{:S(2)}) collective-permute-start(bf16[64,8,256]{2,1,0:T(8,128)(2,1)S(1)} %bitcast.11), channel_id=1, source_target_pairs={{0,16},{8,24},{16,0},{24,8},{1,17},{9,25},{17,1},{25,9},{2,18},{10... | collective-permute-start | bytes 786440 | tf_op jit(solution)/shard_map/ppermute | solution.py:426
  29.0 0.0 collective-permute-done.refs_1_
  29.0 0.0 copy-done.3
  29.0 7.2 %products.1 = (bf16[16,384,256]{2,1,0:T(8,128)(2,1)S(1)}, bf16[16,384,256]{2,1,0:T(8,128)(2,1)S(1)}) custom-call(f32[8,2,384]{2,1,0:T(2,128)S(1)} %copy-done.3, bf16[64,8,256]{2,1,0:T(8,128)(2,1)S(1)} %bitcast.12, bf16[64,8,256]{2,1,0:T(8,128)(2,1)S(1)} %collective-permute-done.refs_1_, bf16[32,32,16,384]{3,2,1,0:T(8,128)(2,1)} %table.1.refs_2_.refs_3_), custom_call_target="tpu_custom_call" | custom-call | flops 1610612736 | bytes 20971520 | tf_op jit(solution)/shard_map/products/pallas_call | solution.py:291
  36.2 0.0 collective-permute-done.1.refs_0_
  36.2 0.1 collective-permute-start.2
  36.3 1.5 %collective-permute-done.2.refs_1_ = bf16[64,8,256]{2,1,0:T(8,128)(2,1)S(1)} collective-permute-done((bf16[64,8,256]{2,1,0:T(8,128)(2,1)S(1)}, bf16[64,8,256]{2,1,0:T(8,128)(2,1)S(1)}, u32[]{:S(2)}, u32[]{:S(2)}) %collective-permute-start.2) | collective-permute-done | bytes 262176 | tf_op jit(solution)/shard_map/ppermute | solution.py:426
  37.8 0.0 copy-done.4
  37.8 25.1 %combine.1 = bf16[8,16,2,384,256]{4,3,2,1,0:T(8,128)(2,1)} custom-call(s32[2]{0:T(128)S(1)} %copy-done.4, bf16[64,8,256]{2,1,0:T(8,128)(2,1)S(1)} %collective-permute-done.1.refs_0_, bf16[64,8,256]{2,1,0:T(8,128)(2,1)S(1)} %collective-permute-done.2.refs_1_, bf16[16,384,256]{2,1,0:T(8,128)(2,1)S(1)} %get-tuple-element.15.refs_2_, ...), custom_call_target="tpu_custom_call" | custom-call | tf_op jit(solution)/shard_map/combine/pallas_call | solution.py:384
Async XLA Ops:
  0.0 1.2 %copy-start = (f32[16,2,8192]{2,1,0:T(2,128)S(1)}, f32[16,2,8192]{2,1,0:T(2,128)}, u32[]{:S(2)}) copy-start(f32[16,2,8192]{2,1,0:T(2,128)} %param.5) | copy-start | bytes 3145732
  1.2 1.0 %copy-start.1 = (bf16[1536,128]{1,0:T(8,128)(2,1)S(1)}, bf16[1536,128]{1,0:T(8,128)(2,1)}, u32[]{:S(2)}) copy-start(bf16[1536,128]{1,0:T(8,128)(2,1)} %constant.10.clone.refs_1_) | copy-start | bytes 1179652
  2.2 0.7 %copy-start.2 = (s32[2048]{0:T(1024)S(1)}, s32[2048]{0:T(1024)}, u32[]{:S(2)}) copy-start(s32[2048]{0:T(1024)} %param.7) | copy-start | bytes 24580
  8.6 18.3 %all-to-all-start = ((bf16[32,16,256]{2,1,0:T(8,128)(2,1)}), bf16[32,16,256]{2,1,0:T(8,128)(2,1)S(1)}, u32[]{:S(2)}, u32[]{:S(2)}) async-start(bf16[32,16,256]{2,1,0:T(8,128)(2,1)} %bitcast.6), calls=%async_computation | async-start | bytes 524288 | tf_op jit(solution)/shard_map/all_to_all | solution.py:420
  16.5 12.5 %copy-start.3 = (f32[8,2,384]{2,1,0:T(2,128)S(1)}, f32[8,2,384]{2,1,0:T(2,128)}, u32[]{:S(2)}) copy-start(f32[8,2,384]{2,1,0:T(2,128)} %kern_ref.1) | copy-start | bytes 73732
  26.9 10.9 %copy-start.4 = (s32[2]{0:T(128)S(1)}, s32[2]{0:T(128)}, u32[]{:S(2)}) copy-start(s32[2]{0:T(128)} %pad_add_fusion.info_ref) | copy-start | bytes 28
  27.0 2.0 %collective-permute-start = (bf16[64,8,256]{2,1,0:T(8,128)(2,1)S(1)}, bf16[64,8,256]{2,1,0:T(8,128)(2,1)S(1)}, u32[]{:S(2)}, u32[]{:S(2)}) collective-permute-start(bf16[64,8,256]{2,1,0:T(8,128)(2,1)S(1)} %bitcast.10), channel_id=1, source_target_pairs={{0,8},{8,0},{16,24},{24,16},{1,9},{9,1},{17,25},{25,17},{2,10},{10... | collective-permute-start | bytes 786440 | tf_op jit(solution)/shard_map/ppermute | solution.py:426
  27.3 8.9 %collective-permute-start.1 = (bf16[64,8,256]{2,1,0:T(8,128)(2,1)S(1)}, bf16[64,8,256]{2,1,0:T(8,128)(2,1)S(1)}, u32[]{:S(2)}, u32[]{:S(2)}) collective-permute-start(bf16[64,8,256]{2,1,0:T(8,128)(2,1)S(1)} %bitcast.11), channel_id=1, source_target_pairs={{0,16},{8,24},{16,0},{24,8},{1,17},{9,25},{17,1},{25,9},{2,18},{10... | collective-permute-start | bytes 786440 | tf_op jit(solution)/shard_map/ppermute | solution.py:426
  36.2 1.6 %collective-permute-start.2 = (bf16[64,8,256]{2,1,0:T(8,128)(2,1)S(1)}, bf16[64,8,256]{2,1,0:T(8,128)(2,1)S(1)}, u32[]{:S(2)}, u32[]{:S(2)}) collective-permute-start(bf16[64,8,256]{2,1,0:T(8,128)(2,1)S(1)} %collective-permute-done.1.refs_0_), channel_id=1, source_target_pairs={{0,8},{8,0},{16,24},{24,16},{1,9},{9,1},{17,25},{25,17},{2,10},{10... | collective-permute-start | bytes 786440 | tf_op jit(solution)/shard_map/ppermute | solution.py:426

commit v4 on v3

--- a/solution.py
+++ b/solution.py
@@ -53,8 +53,17 @@
     return np.concatenate([table.reshape(-1, LANES) for table in tables])
 
 
-def spectrum_body(ids_ref, *refs):
-    sky_ref, table_ref, out_ref, rows_ref = refs
+def spectrum_body(*refs):
+    sources = refs[:3]
+    out_ref, rows_ref, ids_ref, table_ref, sky_ref, sem = refs[3:]
+    copies = [
+        pltpu.make_async_copy(source, target, sem.at[i])
+        for i, (source, target) in enumerate(zip(sources, (ids_ref, table_ref, sky_ref)))
+    ]
+    for copy in copies:
+        copy.start()
+    for copy in copies:
+        copy.wait()
     maps_count, rows, _ = sky_ref.shape
     owners, groups, cycle_count, lines, slots = out_ref.shape
     outer = rows // cycle_count
@@ -122,10 +131,17 @@
         out_shape=jax.ShapeDtypeStruct(
             (owners, groups, cycle_count, maps_count * 2 // owners, slots), BF16
         ),
-        scratch_shapes=[pltpu.VMEM((maps_count * 2 * high, LANES), F32)],
-        compiler_params=pltpu.CompilerParams(vmem_limit_bytes=20 << 20),
+        in_specs=[pl.BlockSpec(memory_space=pl.ANY)] * 3,
+        scratch_shapes=[
+            pltpu.VMEM((maps_count * 2 * high, LANES), F32),
+            pltpu.VMEM((1, orders), jnp.int32),
+            pltpu.VMEM(tables.shape, BF16),
+            pltpu.VMEM(sky.shape, F32),
+            pltpu.SemaphoreType.DMA((3,)),
+        ],
+        compiler_params=pltpu.CompilerParams(vmem_limit_bytes=60 << 20),
         name="spectrum",
-    )(order_of_slot.reshape(1, orders), sky, jnp.asarray(tables))
+    )(order_of_slot.reshape(1, orders), jnp.asarray(tables), sky)
 
 
 def table_body(info_ref, ids_ref, wig_hbm, out_hbm, wig_ref, out_ref, in_sem, out_sem):
@@ -247,7 +263,7 @@
 
 def products_body(pieces, kern_ref, *refs):
     parts = refs[:pieces]
-    tab_hbm, out_ref, wide_ref, xs, dp, ht, tab_ref, sem = refs[pieces:]
+    tab_hbm, out_ref, wide_ref, tab_ref, xs, dp, ht, sem = refs[pieces:]
     per = parts[0].shape[1]
     lines, degs, slots = out_ref.shape
     chunks = sem.shape[0]
@@ -291,14 +307,15 @@
     return pl.pallas_call(
         functools.partial(products_body, len(parts)),
         in_specs=[whole] * (len(parts) + 1) + [pl.BlockSpec(memory_space=pl.ANY)],
-        out_specs=[whole, whole],
+        out_specs=[whole, whole, whole],
         out_shape=[
             jax.ShapeDtypeStruct((lines, degs, slots), BF16),
             jax.ShapeDtypeStruct((kernel.shape[0] * 2, degs, slots), BF16),
+            jax.ShapeDtypeStruct(table.shape, BF16),
         ],
         scratch_shapes=scratch(len(parts), cycles, per, slots, degs)
-        + [pltpu.VMEM(table.shape, BF16), pltpu.SemaphoreType.DMA((8,))],
-        compiler_params=pltpu.CompilerParams(vmem_limit_bytes=40 << 20),
+        + [pltpu.SemaphoreType.DMA((8,))],
+        compiler_params=pltpu.CompilerParams(vmem_limit_bytes=28 << 20),
         cost_estimate=pl.CostEstimate(
             flops=2 * lines * 8 * cycles * slots * degs, bytes_accessed=20 << 20, transcendentals=0
         ),
@@ -308,7 +325,7 @@
 
 def combine_body(pieces, ready, info_ref, *refs):
     parts = refs[:pieces]
-    held_ref, tab_hbm, wide_ref, out_ref, xs, dp, ht, ab, tab_ref, sem = refs[pieces:]
+    held_ref, tab_ref, wide_ref, out_ref, xs, dp, ht, ab = refs[pieces:]
     per = parts[0].shape[1]
     groups, pairs = dp.shape[:2]
     degs = tab_ref.shape[3]
@@ -319,16 +336,9 @@
     each = pl.cdiv(pairs, early)
     some = pl.cdiv(groups, late)
 
-    fetch = pltpu.make_async_copy(tab_hbm, tab_ref, sem.at[0])
-
     @pl.when(m == 0)
     def _():
-        fetch.start()
         stage(parts, xs)
-
-    @pl.when(m == early)
-    def _():
-        fetch.wait()
 
     @pl.when(m < early)
     def _():
@@ -391,19 +401,15 @@
                 pl.BlockSpec(
                     (2, degs, slots), lambda m, info: (jnp.minimum(m, ready - 1), 0, 0)
                 ),
-                pl.BlockSpec(memory_space=pl.ANY),
+                whole,
                 whole,
             ],
             out_specs=pl.BlockSpec((count, 1, 2, degs, slots), out_index),
             scratch_shapes=scratch(len(parts), cycles, per, slots, degs)
-            + [
-                pltpu.VMEM((2, degs, slots), BF16),
-                pltpu.VMEM(table.shape, BF16),
-                pltpu.SemaphoreType.DMA((1,)),
-            ],
+            + [pltpu.VMEM((2, degs, slots), BF16)],
         ),
         out_shape=jax.ShapeDtypeStruct((count, maps_count, 2, degs, slots), BF16),
-        compiler_params=pltpu.CompilerParams(vmem_limit_bytes=40 << 20),
+        compiler_params=pltpu.CompilerParams(vmem_limit_bytes=26 << 20),
         name="combine",
     )(info, *parts, held, table, wide)
 
@@ -430,7 +436,7 @@
     while bit > 1:
         far = far + [swap(part, bit) for part in far]
         bit //= 2
-    held, wide = products([mine, swap(mine, 1)], table, kernel)
+    held, wide, table = products([mine, swap(mine, 1)], table, kernel)
     held, *far = lax.optimization_barrier((held, *far[1:]))
     parts = []
     for part in far:

time: 63.3 us -> 57.4 us (0.907)
  Pallas kernels: 48.4 us -> 45.2 us
  local copies, waits for them, and re-layouts: 2.92 us -> 0.01 us
    pallas_call x1, Pallas kernels: 25.1 us -> 21.1 us  [combine(): pl.pallas_call(functools.partial(combine_body, len(parts), ready), grid_s...]
    unnamed x10 -> x4, local copies, waits for them, and re-layouts: 2.92 us -> 0.01 us
    pallas_call x1, Pallas kernels: 5.7 us -> 7.34 us  [make_spectrum(): pl.pallas_call(spectrum_body, out_shape=jax.ShapeDtypeStruct((owners, gro...]
    pallas_call x1, Pallas kernels: 7.23 us -> 6.46 us  [products(): pl.pallas_call(functools.partial(products_body, len(parts)), in_specs=[wh...]
  transfers between devices with their start and end apart: 4 -> 4, of which waited for: 1 -> 2; matrix products, arithmetic and copies ran while one was open for 1% -> 1% of each run, Pallas kernels for 28% -> 29%
where the time goes in v4:
time: 57.4 us; the launch traced here: 57.1 us
  Pallas kernels  45.2 us (79%)
  starting transfers between devices  9.3 us (16%)
  waiting for transfers between devices  1.88 us (3%)
  other arithmetic  0.65 us (1%)
    pallas_call x1, Pallas kernels, combine(): pl.pallas_call(functools.partial(combine_body, len(parts), ready), grid_s...  21.1 us
    pallas_call x1, Pallas kernels, make_table(): pl.pallas_call(table_body, in_specs=[pl.BlockSpec(memory_space=pltpu.SMEM...  10.4 us
    pallas_call x1, Pallas kernels, make_spectrum(): pl.pallas_call(spectrum_body, out_shape=jax.ShapeDtypeStruct((owners, gro...  7.34 us
    all_to_all x1, starting transfers between devices, local(): lax.all_to_all(by_owner, ('blk', 'order'), split_axis=0, concat_axis=0, t...  7.3 us
    pallas_call x1, Pallas kernels, products(): pl.pallas_call(functools.partial(products_body, len(parts)), in_specs=[wh...  6.46 us
    ppermute x3, starting transfers between devices, swap(): return lax.ppermute(part, 'blk', [(i, i ^ bit) for i in range(owners)])  2 us
    ppermute x3, waiting for transfers between devices, swap(): return lax.ppermute(part, 'blk', [(i, i ^ bit) for i in range(owners)])  1.87 us
  transfers between devices with their start and end apart: 4, of which 2 were waited for; matrix products, arithmetic and copies ran while one was open for 1% of the time, Pallas kernels for 29%

profile of v4, /device:TPU:0, one launch (start us, length us, event | category | flops | bytes accessed | tf_op | source)
XLA Modules:
  0.0 57.1 jit_solution(11444874939287064890)
XLA Ops:
  0.0 7.3 %spectrum.1 = bf16[4,8,2,8,256]{4,3,2,1,0:T(8,128)(2,1)} custom-call(s32[1,2048]{1,0:T(1,128)} %bitcast.15, bf16[1536,128]{1,0:T(8,128)(2,1)} %constant.10.clone.refs_1_, f32[16,128,128]{2,1,0:T(8,128)} %bitcast.13), custom_call_target="tpu_custom_call" | custom-call | tf_op jit(solution)/shard_map/spectrum/pallas_call | solution.py:129
  7.3 7.3 %all-to-all-start = ((bf16[32,16,256]{2,1,0:T(8,128)(2,1)}), bf16[32,16,256]{2,1,0:T(8,128)(2,1)S(1)}, u32[]{:S(2)}, u32[]{:S(2)}) async-start(bf16[32,16,256]{2,1,0:T(8,128)(2,1)} %bitcast.14), calls=%async_computation | async-start | bytes 524288 | tf_op jit(solution)/shard_map/all_to_all | solution.py:426
  14.7 0.6 %pad_add_fusion.info_ref = s32[2]{0:T(128)} fusion(s32[1]{0:T(128)} %bitcast.1, s32[1]{0:T(128)} %bitcast), kind=kLoop, calls=%fused_computation | loop fusion | flops 2 | bytes 16 | tf_op jit(solution)/shard_map/stack | solution.py:422
  15.3 0.0 copy-start
  15.3 10.4 %table.1.refs_2_ = bf16[32,32,16,384]{3,2,1,0:T(8,128)(2,1)} custom-call(s32[2]{0:T(128)} %pad_add_fusion.info_ref, s32[1,2048]{1,0:T(1,128)} %bitcast.16, bf16[64,384,256]{2,1,0:T(8,128)(2,1)} %wig_hbm.1), custom_call_target="tpu_custom_call" | custom-call | flops 100663296 | bytes 25165824 | tf_op jit(solution)/shard_map/table/pallas_call | solution.py:187
  25.7 0.0 copy-start.1
  25.7 0.0 all-to-all-done
  25.7 0.3 collective-permute-start
  26.0 1.7 %collective-permute-start.1 = (bf16[64,8,256]{2,1,0:T(8,128)(2,1)S(1)}, bf16[64,8,256]{2,1,0:T(8,128)(2,1)S(1)}, u32[]{:S(2)}, u32[]{:S(2)}) collective-permute-start(bf16[64,8,256]{2,1,0:T(8,128)(2,1)S(1)} %bitcast.11), channel_id=1, source_target_pairs={{0,16},{8,24},{16,0},{24,8},{1,17},{9,25},{17,1},{25,9},{2,18},{10... | collective-permute-start | bytes 786440 | tf_op jit(solution)/shard_map/ppermute | solution.py:432
  27.7 0.0 collective-permute-done.refs_1_
  27.7 0.0 copy-done
  27.7 6.5 %products.1 = (bf16[16,384,256]{2,1,0:T(8,128)(2,1)S(1)}, bf16[16,384,256]{2,1,0:T(8,128)(2,1)S(1)}, bf16[32,32,16,384]{3,2,1,0:T(8,128)(2,1)S(1)}) custom-call(f32[8,2,384]{2,1,0:T(2,128)S(1)} %copy-done, bf16[64,8,256]{2,1,0:T(8,128)(2,1)S(1)} %bitcast.12, bf16[64,8,256]{2,1,0:T(8,128)(2,1)S(1)} %collective-permute-done.refs_1_, ...), custom_call_target="tpu_custom_call" | custom-call | flops 1610612736 | bytes 20971520 | tf_op jit(solution)/shard_map/products/pallas_call | solution.py:307
  34.2 0.3 collective-permute-done.1.refs_0_
  34.5 0.0 collective-permute-start.2
  34.5 1.5 %collective-permute-done.2.refs_1_ = bf16[64,8,256]{2,1,0:T(8,128)(2,1)S(1)} collective-permute-done((bf16[64,8,256]{2,1,0:T(8,128)(2,1)S(1)}, bf16[64,8,256]{2,1,0:T(8,128)(2,1)S(1)}, u32[]{:S(2)}, u32[]{:S(2)}) %collective-permute-start.2) | collective-permute-done | bytes 262176 | tf_op jit(solution)/shard_map/ppermute | solution.py:432
  36.1 0.0 copy-done.1
  36.1 21.1 %combine.1 = bf16[8,16,2,384,256]{4,3,2,1,0:T(8,128)(2,1)} custom-call(s32[2]{0:T(128)S(1)} %copy-done.1, bf16[64,8,256]{2,1,0:T(8,128)(2,1)S(1)} %collective-permute-done.1.refs_0_, bf16[64,8,256]{2,1,0:T(8,128)(2,1)S(1)} %collective-permute-done.2.refs_1_, bf16[16,384,256]{2,1,0:T(8,128)(2,1)S(1)} %get-tuple-element.16.refs_2_, ...), custom_call_target="tpu_custom_call" | custom-call | tf_op jit(solution)/shard_map/combine/pallas_call | solution.py:394
Async XLA Ops:
  7.3 18.4 %all-to-all-start = ((bf16[32,16,256]{2,1,0:T(8,128)(2,1)}), bf16[32,16,256]{2,1,0:T(8,128)(2,1)S(1)}, u32[]{:S(2)}, u32[]{:S(2)}) async-start(bf16[32,16,256]{2,1,0:T(8,128)(2,1)} %bitcast.14), calls=%async_computation | async-start | bytes 524288 | tf_op jit(solution)/shard_map/all_to_all | solution.py:426
  15.3 12.4 %copy-start = (f32[8,2,384]{2,1,0:T(2,128)S(1)}, f32[8,2,384]{2,1,0:T(2,128)}, u32[]{:S(2)}) copy-start(f32[8,2,384]{2,1,0:T(2,128)} %kern_ref.1) | copy-start | bytes 73732
  25.7 10.4 %copy-start.1 = (s32[2]{0:T(128)S(1)}, s32[2]{0:T(128)}, u32[]{:S(2)}) copy-start(s32[2]{0:T(128)} %pad_add_fusion.info_ref) | copy-start | bytes 28
  25.7 2.0 %collective-permute-start = (bf16[64,8,256]{2,1,0:T(8,128)(2,1)S(1)}, bf16[64,8,256]{2,1,0:T(8,128)(2,1)S(1)}, u32[]{:S(2)}, u32[]{:S(2)}) collective-permute-start(bf16[64,8,256]{2,1,0:T(8,128)(2,1)S(1)} %bitcast.10), channel_id=1, source_target_pairs={{0,8},{8,0},{16,24},{24,16},{1,9},{9,1},{17,25},{25,17},{2,10},{10... | collective-permute-start | bytes 786440 | tf_op jit(solution)/shard_map/ppermute | solution.py:432
  26.0 8.5 %collective-permute-start.1 = (bf16[64,8,256]{2,1,0:T(8,128)(2,1)S(1)}, bf16[64,8,256]{2,1,0:T(8,128)(2,1)S(1)}, u32[]{:S(2)}, u32[]{:S(2)}) collective-permute-start(bf16[64,8,256]{2,1,0:T(8,128)(2,1)S(1)} %bitcast.11), channel_id=1, source_target_pairs={{0,16},{8,24},{16,0},{24,8},{1,17},{9,25},{17,1},{25,9},{2,18},{10... | collective-permute-start | bytes 786440 | tf_op jit(solution)/shard_map/ppermute | solution.py:432
  34.5 1.5 %collective-permute-start.2 = (bf16[64,8,256]{2,1,0:T(8,128)(2,1)S(1)}, bf16[64,8,256]{2,1,0:T(8,128)(2,1)S(1)}, u32[]{:S(2)}, u32[]{:S(2)}) collective-permute-start(bf16[64,8,256]{2,1,0:T(8,128)(2,1)S(1)} %collective-permute-done.1.refs_0_), channel_id=1, source_target_pairs={{0,8},{8,0},{16,24},{24,16},{1,9},{9,1},{17,25},{25,17},{2,10},{10... | collective-permute-start | bytes 786440 | tf_op jit(solution)/shard_map/ppermute | solution.py:432

commit v5 on v4

--- a/solution.py
+++ b/solution.py
@@ -87,7 +87,7 @@
         rows_ref[pl.ds(start, 2 * high), :] = done.T[: 2 * high]
         return carry
 
-    lax.fori_loop(0, maps_count, one_map, 0, unroll=4)
+    lax.fori_loop(0, maps_count, one_map, 0, unroll=16)
 
     per = 256 // outer
     total = None
@@ -175,7 +175,7 @@
             out_ref[:, i * (step // 2) + row // 2] = jnp.concatenate(both, axis=1).astype(BF16)
         flush(i).start()
 
-    loop(chunks, 2, one)
+    loop(chunks, 4, one)
     for i in range(chunks):
         flush(i).wait()
 
@@ -323,52 +323,74 @@
     )(kernel, *parts, table)
 
 
+def turn_part(ht, line, js):
+    halves = ht.shape[1] // LANES
+    turned = [ht[line, h * LANES : (h + 1) * LANES, js].T for h in range(halves)]
+    return jnp.concatenate(turned, axis=1).astype(BF16)
+
+
 def combine_body(pieces, ready, info_ref, *refs):
     parts = refs[:pieces]
     held_ref, tab_ref, wide_ref, out_ref, xs, dp, ht, ab = refs[pieces:]
     per = parts[0].shape[1]
     groups, pairs = dp.shape[:2]
-    degs = tab_ref.shape[3]
-    count = out_ref.shape[0]
-    m = pl.program_id(0)
-    early = 2 if ready >= 4 else 1
-    late = max(ready - early, 1)
+    count, both_maps, _, width, _ = out_ref.shape
+    cuts = tab_ref.shape[3] // width
+    jc = pl.program_id(1)
+    step = pl.program_id(0) * cuts + jc
+    total = ready // both_maps * cuts
+    first = 1 if total >= 4 else 0
+    early = max(total // 4, 1)
+    late = total - first - early
     each = pl.cdiv(pairs, early)
     some = pl.cdiv(groups, late)
 
-    @pl.when(m == 0)
+    @pl.when(step == first)
     def _():
         stage(parts, xs)
 
-    @pl.when(m < early)
-    def _():
-        loop(each, 8, lambda i: place(jnp.minimum(m * each + i, pairs - 1), per, xs, dp))
-
-    @pl.when((m >= early) & (m < early + late))
+    @pl.when((step >= first) & (step < first + early))
     def _():
         def one(i):
-            multiply(jnp.minimum((m - early) * some + i, groups - 1), dp, tab_ref, ht)
-
-        loop(some, 6, one)
-
-    @pl.when(m < ready)
+            place(jnp.minimum((step - first) * each + i, pairs - 1), per, xs, dp)
+
+        loop(each, 8, one)
+
+    @pl.when((step >= first + early) & (step < total))
+    def _():
+        def one(i):
+            g = (step - first - early) * some + i
+            multiply(jnp.minimum(g, groups - 1), dp, tab_ref, ht)
+
+        loop(some, 4, one)
+
+    @pl.when(step < total)
     def _():
         ab[...] = held_ref[...]
 
-    @pl.when(m >= ready)
-    def _():
-        for c in range(2):
-            ab[c] = turn(ht, 2 * (m - ready) + c)
-
-    for top in range(0, degs, 16):
-        js = slice(top, top + 16)
-        a = ab[0, js, :]
-        b = ab[1, js, :]
-        for n in range(count):
-            p = wide_ref[2 * n, js, :]
-            q = wide_ref[2 * n + 1, js, :]
-            out_ref[n, 0, 0, js, :] = (a * p + b * q).astype(BF16)
-            out_ref[n, 0, 1, js, :] = (b * p - a * q).astype(BF16)
+    def stream(cut):
+        js = slice(cut * width, (cut + 1) * width)
+
+        @pl.when(step >= total)
+        def _():
+            line = 2 * (both_maps * pl.program_id(0) - ready)
+            for c in range(2 * both_maps):
+                ab[c] = turn_part(ht, line + c, js)
+
+        for top in range(0, width, 16):
+            rows = slice(top, top + 16)
+            wide_rows = slice(cut * width + top, cut * width + top + 16)
+            held = [ab[c, rows, :] for c in range(2 * both_maps)]
+            for n in range(count):
+                p = wide_ref[2 * n, wide_rows, :]
+                q = wide_ref[2 * n + 1, wide_rows, :]
+                for k in range(both_maps):
+                    a, b = held[2 * k], held[2 * k + 1]
+                    out_ref[n, k, 0, rows, :] = (a * p + b * q).astype(BF16)
+                    out_ref[n, k, 1, rows, :] = (b * p - a * q).astype(BF16)
+
+    for i in range(cuts):
+        pl.when(jc == i)(functools.partial(stream, i))
 
 
 def combine(info, parts, held, table, wide, owners):
@@ -378,8 +400,12 @@
     ready = held.shape[0] // 2
     maps_count = ready + per * len(parts) // 2
     each = per // 2
-
-    def out_index(m, info):
+    both_maps = 2 if each % 2 == 0 else 1
+    width = degs
+    last = ready // both_maps - 1
+
+    def out_index(t, jc, info):
+        m = t * both_maps
         piece = m // each
         mask = piece & 1
         far = piece >> 1
@@ -388,28 +414,33 @@
             mask = mask + (far & 1) * bit
             far = far >> 1
             bit //= 2
-        return (0, (mask ^ info[0]) * each + m % each, 0, 0, 0)
+        return (0, (mask ^ info[0]) * (each // both_maps) + m % each // both_maps, 0, jc, 0)
 
     whole = pl.BlockSpec(memory_space=pltpu.VMEM)
     return pl.pallas_call(
         functools.partial(combine_body, len(parts), ready),
         grid_spec=pltpu.PrefetchScalarGridSpec(
             num_scalar_prefetch=1,
-            grid=(maps_count,),
+            grid=(maps_count // both_maps, degs // width),
             in_specs=[whole] * len(parts)
             + [
                 pl.BlockSpec(
-                    (2, degs, slots), lambda m, info: (jnp.minimum(m, ready - 1), 0, 0)
+                    (2 * both_maps, width, slots),
+                    lambda t, jc, info: (
+                        jnp.minimum(t, last),
+                        jnp.where(t > last, degs // width - 1, jc),
+                        0,
+                    ),
                 ),
                 whole,
                 whole,
             ],
-            out_specs=pl.BlockSpec((count, 1, 2, degs, slots), out_index),
+            out_specs=pl.BlockSpec((count, both_maps, 2, width, slots), out_index),
             scratch_shapes=scratch(len(parts), cycles, per, slots, degs)
-            + [pltpu.VMEM((2, degs, slots), BF16)],
+            + [pltpu.VMEM((2 * both_maps, width, slots), BF16)],
         ),
         out_shape=jax.ShapeDtypeStruct((count, maps_count, 2, degs, slots), BF16),
-        compiler_params=pltpu.CompilerParams(vmem_limit_bytes=26 << 20),
+        compiler_params=pltpu.CompilerParams(vmem_limit_bytes=33 << 20),
         name="combine",
     )(info, *parts, held, table, wide)
 

time: 57.4 us -> 54.4 us (0.948)
  Pallas kernels: 45.2 us -> 42 us
    pallas_call x1, Pallas kernels: 21.1 us -> 19.3 us  [combine(): pl.pallas_call(functools.partial(combine_body, len(parts), ready), grid_s...]
    pallas_call x1, Pallas kernels: 7.34 us -> 5.91 us  [make_spectrum(): pl.pallas_call(spectrum_body, out_shape=jax.ShapeDtypeStruct((owners, gro...]
  transfers between devices with their start and end apart: 4 -> 4, of which waited for: 2 -> 2; matrix products, arithmetic and copies ran while one was open for 1% -> 1% of each run, Pallas kernels for 29% -> 31%
where the time goes in v5:
time: 54.4 us; the launch traced here: 54.1 us
  Pallas kernels  42 us (77%)
  starting transfers between devices  9.31 us (17%)
  waiting for transfers between devices  2.04 us (4%)
  other arithmetic  0.65 us (1%)
    pallas_call x1, Pallas kernels, combine(): pl.pallas_call(functools.partial(combine_body, len(parts), ready), grid_s...  19.3 us
    pallas_call x1, Pallas kernels, make_table(): pl.pallas_call(table_body, in_specs=[pl.BlockSpec(memory_space=pltpu.SMEM...  10.4 us
    all_to_all x1, starting transfers between devices, local(): lax.all_to_all(by_owner, ('blk', 'order'), split_axis=0, concat_axis=0, t...  7.48 us
    pallas_call x1, Pallas kernels, products(): pl.pallas_call(functools.partial(products_body, len(parts)), in_specs=[wh...  6.46 us
    pallas_call x1, Pallas kernels, make_spectrum(): pl.pallas_call(spectrum_body, out_shape=jax.ShapeDtypeStruct((owners, gro...  5.91 us
    ppermute x3, waiting for transfers between devices, swap(): return lax.ppermute(part, 'blk', [(i, i ^ bit) for i in range(owners)])  2.04 us
    ppermute x3, starting transfers between devices, swap(): return lax.ppermute(part, 'blk', [(i, i ^ bit) for i in range(owners)])  1.83 us
  transfers between devices with their start and end apart: 4, of which 2 were waited for; matrix products, arithmetic and copies ran while one was open for 1% of the time, Pallas kernels for 31%

profile of v5, /device:TPU:0, one launch (start us, length us, event | category | flops | bytes accessed | tf_op | source)
XLA Modules:
  0.0 54.1 jit_solution(4665569642081420924)
XLA Ops:
  0.0 5.9 %spectrum.1 = bf16[4,8,2,8,256]{4,3,2,1,0:T(8,128)(2,1)} custom-call(s32[1,2048]{1,0:T(1,128)} %bitcast.15, bf16[1536,128]{1,0:T(8,128)(2,1)} %constant.10.clone.refs_1_, f32[16,128,128]{2,1,0:T(8,128)} %bitcast.13), custom_call_target="tpu_custom_call" | custom-call | tf_op jit(solution)/shard_map/spectrum/pallas_call | solution.py:129
  5.9 7.5 %all-to-all-start = ((bf16[32,16,256]{2,1,0:T(8,128)(2,1)}), bf16[32,16,256]{2,1,0:T(8,128)(2,1)S(1)}, u32[]{:S(2)}, u32[]{:S(2)}) async-start(bf16[32,16,256]{2,1,0:T(8,128)(2,1)} %bitcast.14), calls=%async_computation | async-start | bytes 524288 | tf_op jit(solution)/shard_map/all_to_all | solution.py:457
  13.4 0.6 %pad_add_fusion.info_ref = s32[2]{0:T(128)} fusion(s32[1]{0:T(128)} %bitcast.1, s32[1]{0:T(128)} %bitcast), kind=kLoop, calls=%fused_computation | loop fusion | flops 2 | bytes 16 | tf_op jit(solution)/shard_map/stack | solution.py:453
  14.1 0.0 copy-start
  14.1 10.4 %table.1.refs_2_ = bf16[32,32,16,384]{3,2,1,0:T(8,128)(2,1)} custom-call(s32[2]{0:T(128)} %pad_add_fusion.info_ref, s32[1,2048]{1,0:T(1,128)} %bitcast.16, bf16[64,384,256]{2,1,0:T(8,128)(2,1)} %wig_hbm.1), custom_call_target="tpu_custom_call" | custom-call | flops 100663296 | bytes 25165824 | tf_op jit(solution)/shard_map/table/pallas_call | solution.py:187
  24.5 0.0 copy-start.1
  24.5 0.0 all-to-all-done
  24.5 0.1 collective-permute-start
  24.6 1.7 %collective-permute-start.1 = (bf16[64,8,256]{2,1,0:T(8,128)(2,1)S(1)}, bf16[64,8,256]{2,1,0:T(8,128)(2,1)S(1)}, u32[]{:S(2)}, u32[]{:S(2)}) collective-permute-start(bf16[64,8,256]{2,1,0:T(8,128)(2,1)S(1)} %bitcast.11), channel_id=1, source_target_pairs={{0,16},{8,24},{16,0},{24,8},{1,17},{9,25},{17,1},{25,9},{2,18},{10... | collective-permute-start | bytes 786440 | tf_op jit(solution)/shard_map/ppermute | solution.py:463
  26.3 0.0 collective-permute-done.refs_1_
  26.3 0.0 copy-done
  26.3 6.5 %products.1 = (bf16[16,384,256]{2,1,0:T(8,128)(2,1)S(1)}, bf16[16,384,256]{2,1,0:T(8,128)(2,1)S(1)}, bf16[32,32,16,384]{3,2,1,0:T(8,128)(2,1)S(1)}) custom-call(f32[8,2,384]{2,1,0:T(2,128)S(1)} %copy-done, bf16[64,8,256]{2,1,0:T(8,128)(2,1)S(1)} %bitcast.12, bf16[64,8,256]{2,1,0:T(8,128)(2,1)S(1)} %collective-permute-done.refs_1_, ...), custom_call_target="tpu_custom_call" | custom-call | flops 1610612736 | bytes 20971520 | tf_op jit(solution)/shard_map/products/pallas_call | solution.py:307
  32.8 0.5 collective-permute-done.1.refs_0_
  33.3 0.0 collective-permute-start.2
  33.3 1.5 %collective-permute-done.2.refs_1_ = bf16[64,8,256]{2,1,0:T(8,128)(2,1)S(1)} collective-permute-done((bf16[64,8,256]{2,1,0:T(8,128)(2,1)S(1)}, bf16[64,8,256]{2,1,0:T(8,128)(2,1)S(1)}, u32[]{:S(2)}, u32[]{:S(2)}) %collective-permute-start.2) | collective-permute-done | bytes 262176 | tf_op jit(solution)/shard_map/ppermute | solution.py:463
  34.8 0.0 copy-done.1
  34.8 19.3 %combine.1 = bf16[8,16,2,384,256]{4,3,2,1,0:T(8,128)(2,1)} custom-call(s32[2]{0:T(128)S(1)} %copy-done.1, bf16[64,8,256]{2,1,0:T(8,128)(2,1)S(1)} %collective-permute-done.1.refs_0_, bf16[64,8,256]{2,1,0:T(8,128)(2,1)S(1)} %collective-permute-done.2.refs_1_, bf16[16,384,256]{2,1,0:T(8,128)(2,1)S(1)} %get-tuple-element.16.refs_2_, ...), custom_call_target="tpu_custom_call" | custom-call | tf_op jit(solution)/shard_map/combine/pallas_call | solution.py:420
Async XLA Ops:
  5.9 18.5 %all-to-all-start = ((bf16[32,16,256]{2,1,0:T(8,128)(2,1)}), bf16[32,16,256]{2,1,0:T(8,128)(2,1)S(1)}, u32[]{:S(2)}, u32[]{:S(2)}) async-start(bf16[32,16,256]{2,1,0:T(8,128)(2,1)} %bitcast.14), calls=%async_computation | async-start | bytes 524288 | tf_op jit(solution)/shard_map/all_to_all | solution.py:457
  14.1 12.2 %copy-start = (f32[8,2,384]{2,1,0:T(2,128)S(1)}, f32[8,2,384]{2,1,0:T(2,128)}, u32[]{:S(2)}) copy-start(f32[8,2,384]{2,1,0:T(2,128)} %kern_ref.1) | copy-start | bytes 73732
  24.5 10.4 %copy-start.1 = (s32[2]{0:T(128)S(1)}, s32[2]{0:T(128)}, u32[]{:S(2)}) copy-start(s32[2]{0:T(128)} %pad_add_fusion.info_ref) | copy-start | bytes 28
  24.5 1.8 %collective-permute-start = (bf16[64,8,256]{2,1,0:T(8,128)(2,1)S(1)}, bf16[64,8,256]{2,1,0:T(8,128)(2,1)S(1)}, u32[]{:S(2)}, u32[]{:S(2)}) collective-permute-start(bf16[64,8,256]{2,1,0:T(8,128)(2,1)S(1)} %bitcast.10), channel_id=1, source_target_pairs={{0,8},{8,0},{16,24},{24,16},{1,9},{9,1},{17,25},{25,17},{2,10},{10... | collective-permute-start | bytes 786440 | tf_op jit(solution)/shard_map/ppermute | solution.py:463
  24.6 8.7 %collective-permute-start.1 = (bf16[64,8,256]{2,1,0:T(8,128)(2,1)S(1)}, bf16[64,8,256]{2,1,0:T(8,128)(2,1)S(1)}, u32[]{:S(2)}, u32[]{:S(2)}) collective-permute-start(bf16[64,8,256]{2,1,0:T(8,128)(2,1)S(1)} %bitcast.11), channel_id=1, source_target_pairs={{0,16},{8,24},{16,0},{24,8},{1,17},{9,25},{17,1},{25,9},{2,18},{10... | collective-permute-start | bytes 786440 | tf_op jit(solution)/shard_map/ppermute | solution.py:463
  33.3 1.5 %collective-permute-start.2 = (bf16[64,8,256]{2,1,0:T(8,128)(2,1)S(1)}, bf16[64,8,256]{2,1,0:T(8,128)(2,1)S(1)}, u32[]{:S(2)}, u32[]{:S(2)}) collective-permute-start(bf16[64,8,256]{2,1,0:T(8,128)(2,1)S(1)} %collective-permute-done.1.refs_0_), channel_id=1, source_target_pairs={{0,8},{8,0},{16,24},{24,16},{1,9},{9,1},{17,25},{25,17},{2,10},{10... | collective-permute-start | bytes 786440 | tf_op jit(solution)/shard_map/ppermute | solution.py:463

commit v6 on v5

--- a/solution.py
+++ b/solution.py
@@ -144,7 +144,7 @@
     )(order_of_slot.reshape(1, orders), jnp.asarray(tables), sky)
 
 
-def table_body(info_ref, ids_ref, wig_hbm, out_hbm, wig_ref, out_ref, in_sem, out_sem):
+def table_body(ids_ref, wig_hbm, out_hbm, wig_ref, out_ref, in_sem, out_sem):
     rows, degs, slots = wig_ref.shape
     chunks = in_sem.shape[0]
     step = rows // chunks
@@ -159,9 +159,9 @@
 
     for i in range(chunks):
         fetch(i).start()
-    start = pl.multiple_of(info_ref[1] * slots, LANES)
+    start = pl.multiple_of(lax.axis_index("order") * slots, LANES)
     ids = ids_ref[:, pl.ds(start, slots)]
-    degree = DEG_LO + info_ref[0] * degs + lax.broadcasted_iota(jnp.int32, (degs, slots), 0)
+    degree = DEG_LO + lax.axis_index("blk") * degs + lax.broadcasted_iota(jnp.int32, (degs, slots), 0)
     live = degree >= ids
 
     def turned(row):
@@ -180,14 +180,13 @@
         flush(i).wait()
 
 
-def make_table(info, wigner_d, order_of_slot):
+def make_table(wigner_d, order_of_slot):
     cycles, degs, slots = wigner_d.shape
     outside = pl.BlockSpec(memory_space=pl.ANY)
     shape = (slots // 8, cycles // 2, 16, degs)
     return pl.pallas_call(
         table_body,
         in_specs=[
-            pl.BlockSpec(memory_space=pltpu.SMEM),
             pl.BlockSpec(memory_space=pltpu.VMEM),
             outside,
         ],
@@ -204,7 +203,7 @@
             flops=cycles * degs * slots * 16, bytes_accessed=cycles * degs * slots * 4, transcendentals=0
         ),
         name="table",
-    )(info, order_of_slot.reshape(1, -1), wigner_d)
+    )(order_of_slot.reshape(1, -1), wigner_d)
 
 
 def stage(parts, xs):
@@ -329,7 +328,7 @@
     return jnp.concatenate(turned, axis=1).astype(BF16)
 
 
-def combine_body(pieces, ready, info_ref, *refs):
+def combine_body(pieces, ready, *refs):
     parts = refs[:pieces]
     held_ref, tab_ref, wide_ref, out_ref, xs, dp, ht, ab = refs[pieces:]
     per = parts[0].shape[1]
@@ -362,7 +361,7 @@
             g = (step - first - early) * some + i
             multiply(jnp.minimum(g, groups - 1), dp, tab_ref, ht)
 
-        loop(some, 4, one)
+        loop(some, 16, one)
 
     @pl.when(step < total)
     def _():
@@ -393,7 +392,7 @@
         pl.when(jc == i)(functools.partial(stream, i))
 
 
-def combine(info, parts, held, table, wide, owners):
+def combine(parts, held, table, wide, owners):
     cycles, per, slots = parts[0].shape
     degs = table.shape[3]
     count = wide.shape[0] // 2
@@ -404,7 +403,7 @@
     width = degs
     last = ready // both_maps - 1
 
-    def out_index(t, jc, info):
+    def out_index(t, jc):
         m = t * both_maps
         piece = m // each
         mask = piece & 1
@@ -414,19 +413,19 @@
             mask = mask + (far & 1) * bit
             far = far >> 1
             bit //= 2
-        return (0, (mask ^ info[0]) * (each // both_maps) + m % each // both_maps, 0, jc, 0)
+        return (0, (mask ^ lax.axis_index("blk")) * (each // both_maps) + m % each // both_maps, 0, jc, 0)
 
     whole = pl.BlockSpec(memory_space=pltpu.VMEM)
     return pl.pallas_call(
         functools.partial(combine_body, len(parts), ready),
         grid_spec=pltpu.PrefetchScalarGridSpec(
-            num_scalar_prefetch=1,
+            num_scalar_prefetch=0,
             grid=(maps_count // both_maps, degs // width),
             in_specs=[whole] * len(parts)
             + [
                 pl.BlockSpec(
                     (2 * both_maps, width, slots),
-                    lambda t, jc, info: (
+                    lambda t, jc: (
                         jnp.minimum(t, last),
                         jnp.where(t > last, degs // width - 1, jc),
                         0,
@@ -442,7 +441,7 @@
         out_shape=jax.ShapeDtypeStruct((count, maps_count, 2, degs, slots), BF16),
         compiler_params=pltpu.CompilerParams(vmem_limit_bytes=33 << 20),
         name="combine",
-    )(info, *parts, held, table, wide)
+    )(*parts, held, table, wide)
 
 
 def local(sky_maps, wigner_d, order_of_slot, kernel):
@@ -450,12 +449,11 @@
     maps_count, cycle_count, _ = sky_maps.shape
     groups = lax.axis_size("order")
     owners = lax.axis_size("blk")
-    info = jnp.stack([lax.axis_index("blk"), lax.axis_index("order")]).astype(jnp.int32)
     by_owner = make_spectrum(sky_maps, order_of_slot, owners, groups)
     per = maps_count * 2 // owners
     by_owner = by_owner.reshape(owners * groups, cycle_count * per, slot_count)
     mine = lax.all_to_all(by_owner, ("blk", "order"), split_axis=0, concat_axis=0, tiled=True)
-    table = make_table(info, wigner_d, order_of_slot)
+    table = make_table(wigner_d, order_of_slot)
     mine, table = lax.optimization_barrier((mine, table))
     mine = mine.reshape(cycles, per, slot_count)
 
@@ -472,7 +470,7 @@
     parts = []
     for part in far:
         parts += [part, swap(part, 1)]
-    return combine(info, parts, held, table, wide, owners)
+    return combine(parts, held, table, wide, owners)
 
 
 def solution(mesh):

time: 54.4 us -> 52.3 us (0.961)
  Pallas kernels: 42 us -> 40.5 us
  other arithmetic: 0.65 us -> 0 us
    pallas_call x1, Pallas kernels: 19.3 us -> 17.8 us  [combine(): pl.pallas_call(functools.partial(combine_body, len(parts), ready), grid_s...]
    another operation x1 -> x0, other arithmetic: 0.65 us -> none  [local(): jnp.stack([lax.axis_index('blk'), lax.axis_index('order')])]
  transfers between devices with their start and end apart: 4 -> 4, of which waited for: 2 -> 3; matrix products, arithmetic and copies ran while one was open for 1% -> 0% of each run, Pallas kernels for 31% -> 32%
where the time goes in v6:
time: 52.3 us; the launch traced here: 52 us
  Pallas kernels  40.5 us (77%)
  starting transfers between devices  9.15 us (17%)
  waiting for transfers between devices  2.28 us (4%)
    pallas_call x1, Pallas kernels, combine(): pl.pallas_call(functools.partial(combine_body, len(parts), ready), grid_s...  17.8 us
    pallas_call x1, Pallas kernels, make_table(): pl.pallas_call(table_body, in_specs=[pl.BlockSpec(memory_space=pltpu.VMEM...  10.3 us
    all_to_all x1, starting transfers between devices, local(): lax.all_to_all(by_owner, ('blk', 'order'), split_axis=0, concat_axis=0, t...  7.48 us
    pallas_call x1, Pallas kernels, products(): pl.pallas_call(functools.partial(products_body, len(parts)), in_specs=[wh...  6.46 us
    pallas_call x1, Pallas kernels, make_spectrum(): pl.pallas_call(spectrum_body, out_shape=jax.ShapeDtypeStruct((owners, gro...  5.92 us
    ppermute x3, waiting for transfers between devices, swap(): return lax.ppermute(part, 'blk', [(i, i ^ bit) for i in range(owners)])  2.11 us
    ppermute x3, starting transfers between devices, swap(): return lax.ppermute(part, 'blk', [(i, i ^ bit) for i in range(owners)])  1.67 us
  transfers between devices with their start and end apart: 4, of which 3 were waited for; matrix products, arithmetic and copies ran while one was open for 0% of the time, Pallas kernels for 32%

profile of v6, /device:TPU:0, one launch (start us, length us, event | category | flops | bytes accessed | tf_op | source)
XLA Modules:
  0.0 52.0 jit_solution(7193913354050663885)
XLA Ops:
  0.0 5.9 %spectrum.1 = bf16[4,8,2,8,256]{4,3,2,1,0:T(8,128)(2,1)} custom-call(s32[1,2048]{1,0:T(1,128)} %bitcast.13, bf16[1536,128]{1,0:T(8,128)(2,1)} %constant.2.clone.refs_1_, f32[16,128,128]{2,1,0:T(8,128)} %bitcast.11), custom_call_target="tpu_custom_call" | custom-call | tf_op jit(solution)/shard_map/spectrum/pallas_call | solution.py:129
  5.9 7.5 %all-to-all-start = ((bf16[32,16,256]{2,1,0:T(8,128)(2,1)}), bf16[32,16,256]{2,1,0:T(8,128)(2,1)S(1)}, u32[]{:S(2)}, u32[]{:S(2)}) async-start(bf16[32,16,256]{2,1,0:T(8,128)(2,1)} %bitcast.12), calls=%async_computation | async-start | bytes 524288 | tf_op jit(solution)/shard_map/all_to_all | solution.py:455
  13.4 0.0 copy-start
  13.4 10.3 %table.1.refs_2_ = bf16[32,32,16,384]{3,2,1,0:T(8,128)(2,1)} custom-call(s32[1,2048]{1,0:T(1,128)} %bitcast.14, bf16[64,384,256]{2,1,0:T(8,128)(2,1)} %wig_hbm.1), custom_call_target="tpu_custom_call" | custom-call | flops 100663296 | bytes 25165824 | tf_op jit(solution)/shard_map/table/pallas_call | solution.py:187
  23.7 0.2 all-to-all-done
  23.9 0.0 collective-permute-start
  23.9 1.7 %collective-permute-start.1 = (bf16[64,8,256]{2,1,0:T(8,128)(2,1)S(1)}, bf16[64,8,256]{2,1,0:T(8,128)(2,1)S(1)}, u32[]{:S(2)}, u32[]{:S(2)}) collective-permute-start(bf16[64,8,256]{2,1,0:T(8,128)(2,1)S(1)} %bitcast.9), channel_id=1, source_target_pairs={{0,16},{8,24},{16,0},{24,8},{1,17},{9,25},{17,1},{25,9},{2,18},{10... | collective-permute-start | bytes 786440 | tf_op jit(solution)/shard_map/ppermute | solution.py:461
  25.6 0.0 collective-permute-done.refs_1_
  25.6 0.0 copy-done
  25.6 6.5 %products.1 = (bf16[16,384,256]{2,1,0:T(8,128)(2,1)S(1)}, bf16[16,384,256]{2,1,0:T(8,128)(2,1)S(1)}, bf16[32,32,16,384]{3,2,1,0:T(8,128)(2,1)S(1)}) custom-call(f32[8,2,384]{2,1,0:T(2,128)S(1)} %copy-done, bf16[64,8,256]{2,1,0:T(8,128)(2,1)S(1)} %bitcast.10, bf16[64,8,256]{2,1,0:T(8,128)(2,1)S(1)} %collective-permute-done.refs_1_, ...), custom_call_target="tpu_custom_call" | custom-call | flops 1610612736 | bytes 20971520 | tf_op jit(solution)/shard_map/products/pallas_call | solution.py:306
  32.0 0.6 %collective-permute-done.1.refs_0_ = bf16[64,8,256]{2,1,0:T(8,128)(2,1)S(1)} collective-permute-done((bf16[64,8,256]{2,1,0:T(8,128)(2,1)S(1)}, bf16[64,8,256]{2,1,0:T(8,128)(2,1)S(1)}, u32[]{:S(2)}, u32[]{:S(2)}) %collective-permute-start.1) | collective-permute-done | bytes 262176 | tf_op jit(solution)/shard_map/ppermute | solution.py:461
  32.6 0.0 collective-permute-start.2
  32.6 1.5 %collective-permute-done.2.refs_1_ = bf16[64,8,256]{2,1,0:T(8,128)(2,1)S(1)} collective-permute-done((bf16[64,8,256]{2,1,0:T(8,128)(2,1)S(1)}, bf16[64,8,256]{2,1,0:T(8,128)(2,1)S(1)}, u32[]{:S(2)}, u32[]{:S(2)}) %collective-permute-start.2) | collective-permute-done | bytes 262176 | tf_op jit(solution)/shard_map/ppermute | solution.py:461
  34.1 17.8 %combine.1 = bf16[8,16,2,384,256]{4,3,2,1,0:T(8,128)(2,1)} custom-call(bf16[64,8,256]{2,1,0:T(8,128)(2,1)S(1)} %collective-permute-done.1.refs_0_, bf16[64,8,256]{2,1,0:T(8,128)(2,1)S(1)} %collective-permute-done.2.refs_1_, bf16[16,384,256]{2,1,0:T(8,128)(2,1)S(1)} %get-tuple-element.16.refs_2_, bf16[32,32,16,384]{3,2,1,0:T(8,128)(2,1)S(1)} %get-tuple-element.17.refs_3_, ...), custom_call_target="tpu_custom_call" | custom-call | tf_op jit(solution)/shard_map/combine/pallas_call | solution.py:419
Async XLA Ops:
  5.9 18.0 %all-to-all-start = ((bf16[32,16,256]{2,1,0:T(8,128)(2,1)}), bf16[32,16,256]{2,1,0:T(8,128)(2,1)S(1)}, u32[]{:S(2)}, u32[]{:S(2)}) async-start(bf16[32,16,256]{2,1,0:T(8,128)(2,1)} %bitcast.12), calls=%async_computation | async-start | bytes 524288 | tf_op jit(solution)/shard_map/all_to_all | solution.py:455
  13.4 12.1 %copy-start = (f32[8,2,384]{2,1,0:T(2,128)S(1)}, f32[8,2,384]{2,1,0:T(2,128)}, u32[]{:S(2)}) copy-start(f32[8,2,384]{2,1,0:T(2,128)} %kern_ref.1) | copy-start | bytes 73732
  23.9 1.7 %collective-permute-start = (bf16[64,8,256]{2,1,0:T(8,128)(2,1)S(1)}, bf16[64,8,256]{2,1,0:T(8,128)(2,1)S(1)}, u32[]{:S(2)}, u32[]{:S(2)}) collective-permute-start(bf16[64,8,256]{2,1,0:T(8,128)(2,1)S(1)} %bitcast.8), channel_id=1, source_target_pairs={{0,8},{8,0},{16,24},{24,16},{1,9},{9,1},{17,25},{25,17},{2,10},{10... | collective-permute-start | bytes 786440 | tf_op jit(solution)/shard_map/ppermute | solution.py:461
  23.9 8.7 %collective-permute-start.1 = (bf16[64,8,256]{2,1,0:T(8,128)(2,1)S(1)}, bf16[64,8,256]{2,1,0:T(8,128)(2,1)S(1)}, u32[]{:S(2)}, u32[]{:S(2)}) collective-permute-start(bf16[64,8,256]{2,1,0:T(8,128)(2,1)S(1)} %bitcast.9), channel_id=1, source_target_pairs={{0,16},{8,24},{16,0},{24,8},{1,17},{9,25},{17,1},{25,9},{2,18},{10... | collective-permute-start | bytes 786440 | tf_op jit(solution)/shard_map/ppermute | solution.py:461
  32.6 1.5 %collective-permute-start.2 = (bf16[64,8,256]{2,1,0:T(8,128)(2,1)S(1)}, bf16[64,8,256]{2,1,0:T(8,128)(2,1)S(1)}, u32[]{:S(2)}, u32[]{:S(2)}) collective-permute-start(bf16[64,8,256]{2,1,0:T(8,128)(2,1)S(1)} %collective-permute-done.1.refs_0_), channel_id=1, source_target_pairs={{0,8},{8,0},{16,24},{24,16},{1,9},{9,1},{17,25},{25,17},{2,10},{10... | collective-permute-start | bytes 786440 | tf_op jit(solution)/shard_map/ppermute | solution.py:461

commit v7 on v6

--- a/solution.py
+++ b/solution.py
@@ -89,23 +89,33 @@
 
     lax.fori_loop(0, maps_count, one_map, 0, unroll=16)
 
-    per = 256 // outer
-    total = None
-    for block in range(orders // 256):
-        parts = [
+    lines_all = cycle_count * maps_count * 2
+    per = LANES // outer
+    sources_rows = []
+    for block in range(orders // LANES):
+        held = [
             rows_ref[pl.ds(block * per + i, maps_count * 2, stride=high), :] for i in range(per)
         ]
-        left = jnp.concatenate(
-            [
-                jnp.concatenate([part[:, r * outer : (r + 1) * outer] for part in parts], axis=1)
-                for r in range(cycle_count)
-            ],
-            axis=0,
-        ).astype(BF16)
-        order = block * 256 + lax.broadcasted_iota(jnp.int32, (256, orders), 0)
-        pick = jnp.where(order == ids_ref[...], 1.0, 0.0).astype(BF16)
-        term = jnp.dot(left, pick, preferred_element_type=F32)
-        total = term if total is None else total + term
+        sources_rows.append(
+            jnp.concatenate(
+                [
+                    jnp.concatenate([part[:, r * outer : (r + 1) * outer] for part in held], axis=1)
+                    for r in range(cycle_count)
+                ],
+                axis=0,
+            )
+        )
+    tiles = []
+    for t in range(orders // LANES):
+        ids = jnp.broadcast_to(ids_ref[:, t * LANES : (t + 1) * LANES], (lines_all, LANES))
+        lane = ids % LANES
+        where = ids // LANES
+        tile = jnp.zeros((lines_all, LANES), F32)
+        for block, source in enumerate(sources_rows):
+            found = jnp.take_along_axis(source, lane, axis=1, mode="promise_in_bounds")
+            tile = jnp.where(where == block, found, tile)
+        tiles.append(tile)
+    total = jnp.concatenate(tiles, axis=1)
     for k in range(owners):
         picked = [
             total[r * 2 * maps_count + k * lines : r * 2 * maps_count + (k + 1) * lines]

time: 52.3 us -> 51.7 us (0.989)
  Pallas kernels: 40.5 us -> 39.9 us
    pallas_call x1, Pallas kernels: 5.92 us -> 5.29 us  [make_spectrum(): pl.pallas_call(spectrum_body, out_shape=jax.ShapeDtypeStruct((owners, gro...]
  transfers between devices with their start and end apart: 4 -> 4, of which waited for: 3 -> 3; matrix products, arithmetic and copies ran while one was open for 0% -> 0% of each run, Pallas kernels for 32% -> 33%
where the time goes in v7:
time: 51.7 us; the launch traced here: 51.4 us
  Pallas kernels  39.9 us (77%)
  starting transfers between devices  9.15 us (18%)
  waiting for transfers between devices  2.28 us (4%)
    pallas_call x1, Pallas kernels, combine(): pl.pallas_call(functools.partial(combine_body, len(parts), ready), grid_s...  17.8 us
    pallas_call x1, Pallas kernels, make_table(): pl.pallas_call(table_body, in_specs=[pl.BlockSpec(memory_space=pltpu.VMEM...  10.3 us
    all_to_all x1, starting transfers between devices, local(): lax.all_to_all(by_owner, ('blk', 'order'), split_axis=0, concat_axis=0, t...  7.48 us
    pallas_call x1, Pallas kernels, products(): pl.pallas_call(functools.partial(products_body, len(parts)), in_specs=[wh...  6.46 us
    pallas_call x1, Pallas kernels, make_spectrum(): pl.pallas_call(spectrum_body, out_shape=jax.ShapeDtypeStruct((owners, gro...  5.29 us
    ppermute x3, waiting for transfers between devices, swap(): return lax.ppermute(part, 'blk', [(i, i ^ bit) for i in range(owners)])  2.11 us
    ppermute x3, starting transfers between devices, swap(): return lax.ppermute(part, 'blk', [(i, i ^ bit) for i in range(owners)])  1.67 us
  transfers between devices with their start and end apart: 4, of which 3 were waited for; matrix products, arithmetic and copies ran while one was open for 0% of the time, Pallas kernels for 33%

profile of v7, /device:TPU:0, one launch (start us, length us, event | category | flops | bytes accessed | tf_op | source)
XLA Modules:
  0.0 51.4 jit_solution(14363407104356147788)
XLA Ops:
  0.0 5.3 %spectrum.1 = bf16[4,8,2,8,256]{4,3,2,1,0:T(8,128)(2,1)} custom-call(s32[1,2048]{1,0:T(1,128)} %bitcast.13, bf16[1536,128]{1,0:T(8,128)(2,1)} %constant.2.clone.refs_1_, f32[16,128,128]{2,1,0:T(8,128)} %bitcast.11), custom_call_target="tpu_custom_call" | custom-call | tf_op jit(solution)/shard_map/spectrum/pallas_call | solution.py:139
  5.3 7.5 %all-to-all-start = ((bf16[32,16,256]{2,1,0:T(8,128)(2,1)}), bf16[32,16,256]{2,1,0:T(8,128)(2,1)S(1)}, u32[]{:S(2)}, u32[]{:S(2)}) async-start(bf16[32,16,256]{2,1,0:T(8,128)(2,1)} %bitcast.12), calls=%async_computation | async-start | bytes 524288 | tf_op jit(solution)/shard_map/all_to_all | solution.py:465
  12.8 0.0 copy-start
  12.8 10.3 %table.1.refs_2_ = bf16[32,32,16,384]{3,2,1,0:T(8,128)(2,1)} custom-call(s32[1,2048]{1,0:T(1,128)} %bitcast.14, bf16[64,384,256]{2,1,0:T(8,128)(2,1)} %wig_hbm.1), custom_call_target="tpu_custom_call" | custom-call | flops 100663296 | bytes 25165824 | tf_op jit(solution)/shard_map/table/pallas_call | solution.py:197
  23.1 0.2 all-to-all-done
  23.3 0.0 collective-permute-start
  23.3 1.7 %collective-permute-start.1 = (bf16[64,8,256]{2,1,0:T(8,128)(2,1)S(1)}, bf16[64,8,256]{2,1,0:T(8,128)(2,1)S(1)}, u32[]{:S(2)}, u32[]{:S(2)}) collective-permute-start(bf16[64,8,256]{2,1,0:T(8,128)(2,1)S(1)} %bitcast.9), channel_id=1, source_target_pairs={{0,16},{8,24},{16,0},{24,8},{1,17},{9,25},{17,1},{25,9},{2,18},{10... | collective-permute-start | bytes 786440 | tf_op jit(solution)/shard_map/ppermute | solution.py:471
  24.9 0.0 collective-permute-done.refs_1_
  24.9 0.0 copy-done
  24.9 6.5 %products.1 = (bf16[16,384,256]{2,1,0:T(8,128)(2,1)S(1)}, bf16[16,384,256]{2,1,0:T(8,128)(2,1)S(1)}, bf16[32,32,16,384]{3,2,1,0:T(8,128)(2,1)S(1)}) custom-call(f32[8,2,384]{2,1,0:T(2,128)S(1)} %copy-done, bf16[64,8,256]{2,1,0:T(8,128)(2,1)S(1)} %bitcast.10, bf16[64,8,256]{2,1,0:T(8,128)(2,1)S(1)} %collective-permute-done.refs_1_, ...), custom_call_target="tpu_custom_call" | custom-call | flops 1610612736 | bytes 20971520 | tf_op jit(solution)/shard_map/products/pallas_call | solution.py:316
  31.4 0.6 %collective-permute-done.1.refs_0_ = bf16[64,8,256]{2,1,0:T(8,128)(2,1)S(1)} collective-permute-done((bf16[64,8,256]{2,1,0:T(8,128)(2,1)S(1)}, bf16[64,8,256]{2,1,0:T(8,128)(2,1)S(1)}, u32[]{:S(2)}, u32[]{:S(2)}) %collective-permute-start.1) | collective-permute-done | bytes 262176 | tf_op jit(solution)/shard_map/ppermute | solution.py:471
  32.0 0.0 collective-permute-start.2
  32.0 1.5 %collective-permute-done.2.refs_1_ = bf16[64,8,256]{2,1,0:T(8,128)(2,1)S(1)} collective-permute-done((bf16[64,8,256]{2,1,0:T(8,128)(2,1)S(1)}, bf16[64,8,256]{2,1,0:T(8,128)(2,1)S(1)}, u32[]{:S(2)}, u32[]{:S(2)}) %collective-permute-start.2) | collective-permute-done | bytes 262176 | tf_op jit(solution)/shard_map/ppermute | solution.py:471
  33.5 17.8 %combine.1 = bf16[8,16,2,384,256]{4,3,2,1,0:T(8,128)(2,1)} custom-call(bf16[64,8,256]{2,1,0:T(8,128)(2,1)S(1)} %collective-permute-done.1.refs_0_, bf16[64,8,256]{2,1,0:T(8,128)(2,1)S(1)} %collective-permute-done.2.refs_1_, bf16[16,384,256]{2,1,0:T(8,128)(2,1)S(1)} %get-tuple-element.16.refs_2_, bf16[32,32,16,384]{3,2,1,0:T(8,128)(2,1)S(1)} %get-tuple-element.17.refs_3_, ...), custom_call_target="tpu_custom_call" | custom-call | tf_op jit(solution)/shard_map/combine/pallas_call | solution.py:429
Async XLA Ops:
  5.3 18.0 %all-to-all-start = ((bf16[32,16,256]{2,1,0:T(8,128)(2,1)}), bf16[32,16,256]{2,1,0:T(8,128)(2,1)S(1)}, u32[]{:S(2)}, u32[]{:S(2)}) async-start(bf16[32,16,256]{2,1,0:T(8,128)(2,1)} %bitcast.12), calls=%async_computation | async-start | bytes 524288 | tf_op jit(solution)/shard_map/all_to_all | solution.py:465
  12.8 12.1 %copy-start = (f32[8,2,384]{2,1,0:T(2,128)S(1)}, f32[8,2,384]{2,1,0:T(2,128)}, u32[]{:S(2)}) copy-start(f32[8,2,384]{2,1,0:T(2,128)} %kern_ref.1) | copy-start | bytes 73732
  23.3 1.7 %collective-permute-start = (bf16[64,8,256]{2,1,0:T(8,128)(2,1)S(1)}, bf16[64,8,256]{2,1,0:T(8,128)(2,1)S(1)}, u32[]{:S(2)}, u32[]{:S(2)}) collective-permute-start(bf16[64,8,256]{2,1,0:T(8,128)(2,1)S(1)} %bitcast.8), channel_id=1, source_target_pairs={{0,8},{8,0},{16,24},{24,16},{1,9},{9,1},{17,25},{25,17},{2,10},{10... | collective-permute-start | bytes 786440 | tf_op jit(solution)/shard_map/ppermute | solution.py:471
  23.3 8.7 %collective-permute-start.1 = (bf16[64,8,256]{2,1,0:T(8,128)(2,1)S(1)}, bf16[64,8,256]{2,1,0:T(8,128)(2,1)S(1)}, u32[]{:S(2)}, u32[]{:S(2)}) collective-permute-start(bf16[64,8,256]{2,1,0:T(8,128)(2,1)S(1)} %bitcast.9), channel_id=1, source_target_pairs={{0,16},{8,24},{16,0},{24,8},{1,17},{9,25},{17,1},{25,9},{2,18},{10... | collective-permute-start | bytes 786440 | tf_op jit(solution)/shard_map/ppermute | solution.py:471
  32.0 1.5 %collective-permute-start.2 = (bf16[64,8,256]{2,1,0:T(8,128)(2,1)S(1)}, bf16[64,8,256]{2,1,0:T(8,128)(2,1)S(1)}, u32[]{:S(2)}, u32[]{:S(2)}) collective-permute-start(bf16[64,8,256]{2,1,0:T(8,128)(2,1)S(1)} %collective-permute-done.1.refs_0_), channel_id=1, source_target_pairs={{0,8},{8,0},{16,24},{24,16},{1,9},{9,1},{17,25},{25,17},{2,10},{10... | collective-permute-start | bytes 786440 | tf_op jit(solution)/shard_map/ppermute | solution.py:471

commit v8 on v7

--- a/solution.py
+++ b/solution.py
@@ -107,13 +107,13 @@
         )
     tiles = []
     for t in range(orders // LANES):
-        ids = jnp.broadcast_to(ids_ref[:, t * LANES : (t + 1) * LANES], (lines_all, LANES))
-        lane = ids % LANES
-        where = ids // LANES
-        tile = jnp.zeros((lines_all, LANES), F32)
+        ids = ids_ref[:, t * LANES : (t + 1) * LANES]
+        lane = jnp.broadcast_to(ids & (LANES - 1), (lines_all, LANES))
+        where = jnp.broadcast_to(ids >> (LANES.bit_length() - 1), (lines_all, LANES))
+        tile = None
         for block, source in enumerate(sources_rows):
             found = jnp.take_along_axis(source, lane, axis=1, mode="promise_in_bounds")
-            tile = jnp.where(where == block, found, tile)
+            tile = found if tile is None else jnp.where(where == block, found, tile)
         tiles.append(tile)
     total = jnp.concatenate(tiles, axis=1)
     for k in range(owners):

time: 51.7 us -> 51.7 us (level)
  no operation moved by 1% of the time
where the time goes in v8:
time: 51.7 us; the launch traced here: 51.3 us
  Pallas kernels  39.8 us (77%)
  starting transfers between devices  9.15 us (18%)
  waiting for transfers between devices  2.28 us (4%)
    pallas_call x1, Pallas kernels, combine(): pl.pallas_call(functools.partial(combine_body, len(parts), ready), grid_s...  17.8 us
    pallas_call x1, Pallas kernels, make_table(): pl.pallas_call(table_body, in_specs=[pl.BlockSpec(memory_space=pltpu.VMEM...  10.3 us
    all_to_all x1, starting transfers between devices, local(): lax.all_to_all(by_owner, ('blk', 'order'), split_axis=0, concat_axis=0, t...  7.48 us
    pallas_call x1, Pallas kernels, products(): pl.pallas_call(functools.partial(products_body, len(parts)), in_specs=[wh...  6.46 us
    pallas_call x1, Pallas kernels, make_spectrum(): pl.pallas_call(spectrum_body, out_shape=jax.ShapeDtypeStruct((owners, gro...  5.26 us
    ppermute x3, waiting for transfers between devices, swap(): return lax.ppermute(part, 'blk', [(i, i ^ bit) for i in range(owners)])  2.11 us
    ppermute x3, starting transfers between devices, swap(): return lax.ppermute(part, 'blk', [(i, i ^ bit) for i in range(owners)])  1.67 us
  transfers between devices with their start and end apart: 4, of which 3 were waited for; matrix products, arithmetic and copies ran while one was open for 0% of the time, Pallas kernels for 33%

profile of v8, /device:TPU:0, one launch (start us, length us, event | category | flops | bytes accessed | tf_op | source)
XLA Modules:
  0.0 51.3 jit_solution(450239868767754639)
XLA Ops:
  0.0 5.3 %spectrum.1 = bf16[4,8,2,8,256]{4,3,2,1,0:T(8,128)(2,1)} custom-call(s32[1,2048]{1,0:T(1,128)} %bitcast.13, bf16[1536,128]{1,0:T(8,128)(2,1)} %constant.2.clone.refs_1_, f32[16,128,128]{2,1,0:T(8,128)} %bitcast.11), custom_call_target="tpu_custom_call" | custom-call | tf_op jit(solution)/shard_map/spectrum/pallas_call | solution.py:139
  5.3 7.5 %all-to-all-start = ((bf16[32,16,256]{2,1,0:T(8,128)(2,1)}), bf16[32,16,256]{2,1,0:T(8,128)(2,1)S(1)}, u32[]{:S(2)}, u32[]{:S(2)}) async-start(bf16[32,16,256]{2,1,0:T(8,128)(2,1)} %bitcast.12), calls=%async_computation | async-start | bytes 524288 | tf_op jit(solution)/shard_map/all_to_all | solution.py:465
  12.8 0.0 copy-start
  12.8 10.3 %table.1.refs_2_ = bf16[32,32,16,384]{3,2,1,0:T(8,128)(2,1)} custom-call(s32[1,2048]{1,0:T(1,128)} %bitcast.14, bf16[64,384,256]{2,1,0:T(8,128)(2,1)} %wig_hbm.1), custom_call_target="tpu_custom_call" | custom-call | flops 100663296 | bytes 25165824 | tf_op jit(solution)/shard_map/table/pallas_call | solution.py:197
  23.1 0.2 all-to-all-done
  23.2 0.0 collective-permute-start
  23.2 1.7 %collective-permute-start.1 = (bf16[64,8,256]{2,1,0:T(8,128)(2,1)S(1)}, bf16[64,8,256]{2,1,0:T(8,128)(2,1)S(1)}, u32[]{:S(2)}, u32[]{:S(2)}) collective-permute-start(bf16[64,8,256]{2,1,0:T(8,128)(2,1)S(1)} %bitcast.9), channel_id=1, source_target_pairs={{0,16},{8,24},{16,0},{24,8},{1,17},{9,25},{17,1},{25,9},{2,18},{10... | collective-permute-start | bytes 786440 | tf_op jit(solution)/shard_map/ppermute | solution.py:471
  24.9 0.0 collective-permute-done.refs_1_
  24.9 0.0 copy-done
  24.9 6.5 %products.1 = (bf16[16,384,256]{2,1,0:T(8,128)(2,1)S(1)}, bf16[16,384,256]{2,1,0:T(8,128)(2,1)S(1)}, bf16[32,32,16,384]{3,2,1,0:T(8,128)(2,1)S(1)}) custom-call(f32[8,2,384]{2,1,0:T(2,128)S(1)} %copy-done, bf16[64,8,256]{2,1,0:T(8,128)(2,1)S(1)} %bitcast.10, bf16[64,8,256]{2,1,0:T(8,128)(2,1)S(1)} %collective-permute-done.refs_1_, ...), custom_call_target="tpu_custom_call" | custom-call | flops 1610612736 | bytes 20971520 | tf_op jit(solution)/shard_map/products/pallas_call | solution.py:316
  31.4 0.6 %collective-permute-done.1.refs_0_ = bf16[64,8,256]{2,1,0:T(8,128)(2,1)S(1)} collective-permute-done((bf16[64,8,256]{2,1,0:T(8,128)(2,1)S(1)}, bf16[64,8,256]{2,1,0:T(8,128)(2,1)S(1)}, u32[]{:S(2)}, u32[]{:S(2)}) %collective-permute-start.1) | collective-permute-done | bytes 262176 | tf_op jit(solution)/shard_map/ppermute | solution.py:471
  31.9 0.0 collective-permute-start.2
  32.0 1.5 %collective-permute-done.2.refs_1_ = bf16[64,8,256]{2,1,0:T(8,128)(2,1)S(1)} collective-permute-done((bf16[64,8,256]{2,1,0:T(8,128)(2,1)S(1)}, bf16[64,8,256]{2,1,0:T(8,128)(2,1)S(1)}, u32[]{:S(2)}, u32[]{:S(2)}) %collective-permute-start.2) | collective-permute-done | bytes 262176 | tf_op jit(solution)/shard_map/ppermute | solution.py:471
  33.5 17.8 %combine.1 = bf16[8,16,2,384,256]{4,3,2,1,0:T(8,128)(2,1)} custom-call(bf16[64,8,256]{2,1,0:T(8,128)(2,1)S(1)} %collective-permute-done.1.refs_0_, bf16[64,8,256]{2,1,0:T(8,128)(2,1)S(1)} %collective-permute-done.2.refs_1_, bf16[16,384,256]{2,1,0:T(8,128)(2,1)S(1)} %get-tuple-element.16.refs_2_, bf16[32,32,16,384]{3,2,1,0:T(8,128)(2,1)S(1)} %get-tuple-element.17.refs_3_, ...), custom_call_target="tpu_custom_call" | custom-call | tf_op jit(solution)/shard_map/combine/pallas_call | solution.py:429
Async XLA Ops:
  5.3 18.0 %all-to-all-start = ((bf16[32,16,256]{2,1,0:T(8,128)(2,1)}), bf16[32,16,256]{2,1,0:T(8,128)(2,1)S(1)}, u32[]{:S(2)}, u32[]{:S(2)}) async-start(bf16[32,16,256]{2,1,0:T(8,128)(2,1)} %bitcast.12), calls=%async_computation | async-start | bytes 524288 | tf_op jit(solution)/shard_map/all_to_all | solution.py:465
  12.8 12.1 %copy-start = (f32[8,2,384]{2,1,0:T(2,128)S(1)}, f32[8,2,384]{2,1,0:T(2,128)}, u32[]{:S(2)}) copy-start(f32[8,2,384]{2,1,0:T(2,128)} %kern_ref.1) | copy-start | bytes 73732
  23.2 1.7 %collective-permute-start = (bf16[64,8,256]{2,1,0:T(8,128)(2,1)S(1)}, bf16[64,8,256]{2,1,0:T(8,128)(2,1)S(1)}, u32[]{:S(2)}, u32[]{:S(2)}) collective-permute-start(bf16[64,8,256]{2,1,0:T(8,128)(2,1)S(1)} %bitcast.8), channel_id=1, source_target_pairs={{0,8},{8,0},{16,24},{24,16},{1,9},{9,1},{17,25},{25,17},{2,10},{10... | collective-permute-start | bytes 786440 | tf_op jit(solution)/shard_map/ppermute | solution.py:471
  23.2 8.7 %collective-permute-start.1 = (bf16[64,8,256]{2,1,0:T(8,128)(2,1)S(1)}, bf16[64,8,256]{2,1,0:T(8,128)(2,1)S(1)}, u32[]{:S(2)}, u32[]{:S(2)}) collective-permute-start(bf16[64,8,256]{2,1,0:T(8,128)(2,1)S(1)} %bitcast.9), channel_id=1, source_target_pairs={{0,16},{8,24},{16,0},{24,8},{1,17},{9,25},{17,1},{25,9},{2,18},{10... | collective-permute-start | bytes 786440 | tf_op jit(solution)/shard_map/ppermute | solution.py:471
  31.9 1.5 %collective-permute-start.2 = (bf16[64,8,256]{2,1,0:T(8,128)(2,1)S(1)}, bf16[64,8,256]{2,1,0:T(8,128)(2,1)S(1)}, u32[]{:S(2)}, u32[]{:S(2)}) collective-permute-start(bf16[64,8,256]{2,1,0:T(8,128)(2,1)S(1)} %collective-permute-done.1.refs_0_), channel_id=1, source_target_pairs={{0,8},{8,0},{16,24},{24,16},{1,9},{9,1},{17,25},{25,17},{2,10},{10... | collective-permute-start | bytes 786440 | tf_op jit(solution)/shard_map/ppermute | solution.py:471
